TPU v7x, 512 devices: a whole 4x4x16 slice. The times are simulated.
512 devices in a mesh: section: 16 (over x, y), tp: 32 (over z, core).
Axes of the slice: x: 4, y: 4, z: 16, core: 2. Of those that a mesh axis runs over, the one named last changes fastest.
Arguments:
- sent_act: bfloat16 [16, 512, 8192], P('section', None, 'tp'), may hold values from -60 to 60
- stash: bfloat16 [16, 512, 8192], P('section', None, 'tp'), may hold values from -60 to 60
- grad_back: bfloat16 [16, 512, 8192], P('section', None, 'tp'), may hold values from -6 to 6
- gain: float32 [16, 8192], P('section', 'tp'), may hold values from 0.25 to 1.75
- self_blocks: bfloat16 [16, 2, 6, 8192, 128], P('section', None, None, 'tp'), may hold values from -0.375 to 0.375
- partner_blocks: bfloat16 [16, 2, 6, 8192, 128], P('section', None, None, 'tp'), may hold values from -0.375 to 0.375
- block_mask: int32 [16, 2, 6, 64], P('section', None, None, 'tp'), may hold values 0 or 1
Outputs:
- out_act: bfloat16 [16, 512, 8192], P('section', None, 'tp')
- grad_in: bfloat16 [16, 512, 8192], P('section', None, 'tp')
- grad_self: bfloat16 [16, 2, 6, 8192, 128], P('section', None, None, 'tp')
- grad_partner: bfloat16 [16, 2, 6, 8192, 128], P('section', None, None, 'tp')
- grad_gain: float32 [16, 8192], P('section', 'tp')
All inputs are finite; a program needn't handle non-finite values. No bound on the sum of `block_mask` on one device may be relied on, other than what follows from the above.
Results may differ from a plain program's by a relative error of at most 0.02.
Values may be sent and summed in bfloat16 or wider, within the bound.
A program may use at most 64 MiB of HBM per device.

v0:
```python
import jax
import jax.numpy as jnp
from jax import lax
from jax.sharding import PartitionSpec as P

D = 8192


EPSILON = 1e-05
GELU_C = 0.7978845608028654
GELU_A = 0.044715


def from_partner(value, axis, apart):
    mask = 2**apart
    pairs = [(source, source ^ mask) for source in range(lax.axis_size(axis))]
    return lax.ppermute(value, axis, pairs)


def from_behind(value, axis, steps):
    count = lax.axis_size(axis)
    pairs = [(source, (source + steps) % count) for source in range(count)]
    return lax.ppermute(value, axis, pairs)


def gelu_value(v):
    inner = GELU_C * (v + GELU_A * v * v * v)
    return 0.5 * v * (1.0 + jnp.tanh(inner))


def gelu_slope(v):
    inner = GELU_C * (v + GELU_A * v * v * v)
    tanh_val = jnp.tanh(inner)
    return 0.5 * (1.0 + tanh_val) + 0.5 * v * (1.0 - tanh_val * tanh_val) * GELU_C * (
        1.0 + 3.0 * GELU_A * v * v
    )


def flip_blocks(x, k, axis):
    shape = x.shape
    low = 2**k
    parts = shape[:axis] + (shape[axis] // (2 * low), 2, low) + shape[axis + 1 :]
    return jnp.flip(x.reshape(parts), axis + 1).reshape(shape)


def block_mix(values, weights):
    return jnp.einsum("tlc,lcd->tld", values, weights, preferred_element_type=jnp.float32)


def block_back(grads, weights):
    return jnp.einsum("tld,lcd->tlc", grads, weights, preferred_element_type=jnp.float32)


def block_grad(values, grads):
    return jnp.einsum("tlc,tld->lcd", values, grads, preferred_element_type=jnp.float32)


def normalize(x, gain_row):
    values = x.astype(jnp.float32)
    squares = lax.psum(jnp.sum(values * values, axis=1), "tp")
    scale = lax.rsqrt(squares / D + EPSILON)
    scaled = values * scale[:, None]
    return ((scaled * gain_row[None, :]).astype(jnp.bfloat16), scaled, scale)


def butterfly(values, selfw, partw, mask, local_bits, finish):
    inputs = []
    partners = []
    count = selfw.shape[0]
    for k in range(count):
        if k < local_bits:
            other = flip_blocks(values, k, 1)
        else:
            other = from_partner(values, "tp", k - local_bits)
        inputs.append(values)
        partners.append(other)
        if finish or k + 1 < count:
            mixed = block_mix(values, selfw[k]) + mask[k][None, :, None] * block_mix(
                other, partw[k]
            )
            values = mixed.astype(jnp.bfloat16)
    return (values, inputs, partners)


def butterfly_back(grads, inputs, partners, selfw, partw, mask, local_bits):
    grads_self = []
    grads_part = []
    for k in reversed(range(selfw.shape[0])):
        grads_self.append(block_grad(inputs[k], grads))
        grads_part.append(mask[k][:, None, None] * block_grad(partners[k], grads))
        own = block_back(grads, selfw[k])
        term = mask[k][None, :, None] * block_back(grads, partw[k])
        if k < local_bits:
            back = flip_blocks(term, k, 1)
        else:
            back = from_partner(term, "tp", k - local_bits)
        grads = (own + back).astype(jnp.bfloat16)
    grads_self = grads_self[::-1]
    grads_part = grads_part[::-1]
    return (grads, jnp.stack(grads_self), jnp.stack(grads_part))


def per_device(sent_act, stash, grad_back, gain, self_blocks, partner_blocks, block_mask):
    tokens = sent_act.shape[1]
    width = sent_act.shape[2]
    block = self_blocks.shape[4]
    factors = self_blocks.shape[2]
    local_blocks = width // block
    local_bits = local_blocks.bit_length() - 1
    selfw = self_blocks[0].reshape(2, factors, local_blocks, block, block)
    partw = partner_blocks[0].reshape(2, factors, local_blocks, block, block)
    mask = block_mask[0].astype(jnp.float32)
    gain_row = gain[0]
    arriving = from_behind(sent_act, "section", 1)[0]
    returning = from_behind(grad_back, "section", -1)[0]
    normed, unused_a, unused_b = normalize(arriving, gain_row)
    first_out, unused_c, unused_d = butterfly(
        normed.reshape(tokens, local_blocks, block), selfw[0], partw[0], mask[0], local_bits, True
    )
    hidden = gelu_value(first_out.astype(jnp.float32)).astype(jnp.bfloat16)
    second_out, unused_e, unused_f = butterfly(
        hidden, selfw[1], partw[1], mask[1], local_bits, True
    )
    out_act = (
        arriving.astype(jnp.float32) + second_out.reshape(tokens, width).astype(jnp.float32)
    ).astype(jnp.bfloat16)
    normed_s, scaled_s, scale_s = normalize(stash[0], gain_row)
    first_s, in_first, par_first = butterfly(
        normed_s.reshape(tokens, local_blocks, block), selfw[0], partw[0], mask[0], local_bits, True
    )
    hidden_s = gelu_value(first_s.astype(jnp.float32)).astype(jnp.bfloat16)
    unused_g, in_second, par_second = butterfly(
        hidden_s, selfw[1], partw[1], mask[1], local_bits, False
    )
    grad_hidden, gs_second, gp_second = butterfly_back(
        returning.reshape(tokens, local_blocks, block),
        in_second,
        par_second,
        selfw[1],
        partw[1],
        mask[1],
        local_bits,
    )
    grad_first = (grad_hidden.astype(jnp.float32) * gelu_slope(first_s.astype(jnp.float32))).astype(
        jnp.bfloat16
    )
    grad_normed, gs_first, gp_first = butterfly_back(
        grad_first, in_first, par_first, selfw[0], partw[0], mask[0], local_bits
    )
    du_flat = grad_normed.reshape(tokens, width).astype(jnp.float32)
    grad_gain = jnp.sum(du_flat * scaled_s, axis=0)
    q_val = du_flat * gain_row[None, :]
    corr = lax.psum(jnp.sum(q_val * scaled_s, axis=1), "tp")
    grad_in = (
        returning.astype(jnp.float32) + scale_s[:, None] * (q_val - scaled_s * corr[:, None] / D)
    ).astype(jnp.bfloat16)
    grad_self = (
        jnp.stack([gs_first, gs_second]).reshape(1, 2, factors, width, block).astype(jnp.bfloat16)
    )
    grad_partner = (
        jnp.stack([gp_first, gp_second]).reshape(1, 2, factors, width, block).astype(jnp.bfloat16)
    )
    return (out_act[None], grad_in[None], grad_self, grad_partner, grad_gain[None])


def solution(mesh):
    in_specs = (
        P("section", None, "tp"),
        P("section", None, "tp"),
        P("section", None, "tp"),
        P("section", "tp"),
        P("section", None, None, "tp", None),
        P("section", None, None, "tp", None),
        P("section", None, None, "tp"),
    )
    out_specs = (
        P("section", None, "tp"),
        P("section", None, "tp"),
        P("section", None, None, "tp", None),
        P("section", None, None, "tp", None),
        P("section", "tp"),
    )
    return jax.shard_map(
        per_device, mesh=mesh, in_specs=in_specs, out_specs=out_specs, check_vma=False
    )
```

profile of v0, /device:TPU:1, one launch (start us, length us, event | category | flops | bytes accessed | tf_op | source)
XLA Modules:
  0.0 721.4 jit_solution(15518051651097219515)
XLA Ops:
  1.8 7.7 %collective-permute-start.11 = (bf16[1,512,256]{1,2,0:T(8,128)(2,1)S(1)}, bf16[1,512,256]{1,2,0:T(8,128)(2,1)S(1)}, u32[]{:S(2)}, u32[]{:S(2)}) collective-permute-start(bf16[1,512,256]{1,2,0:T(8,128)(2,1)S(1)} %copy.52), channel_id=1, source_target_pairs={{0,480},{32,0},{64,32},{96,64},{128,96},{160,128},{192,160},{224,1... | collective-permute-start | bytes 786440 | tf_op jit(solution)/shard_map/ppermute | solution.py:23
  10.7 52.7 %psum.22 = f32[512]{0:T(512)S(1)} all-reduce(f32[512]{0:T(512)S(1)} %multiply_reduce_fusion.2), channel_id=1, replica_groups=mesh['section'=16,'tp'=32] {'tp'}, use_global_device_ids=true, to_apply=%region_3.4 | all-reduce | flops 512 | bytes 4096 | tf_op jit(solution)/shard_map/psum | solution.py:60
  65.2 8.8 %collective-permute-start.12 = (f32[512,2,128]{0,2,1:T(8,128)}, f32[512,2,128]{0,2,1:T(8,128)}, u32[]{:S(2)}, u32[]{:S(2)}) collective-permute-start(f32[512,2,128]{0,2,1:T(8,128)} %fusion.34), channel_id=1, source_target_pairs={{0,16},{1,17},{2,18},{3,19},{4,20},{5,21},{6,22},{7,23},{8,24},{9,... | collective-permute-start | bytes 1572872 | tf_op jit(solution)/shard_map/ppermute | solution.py:17
  74.3 2.0 fusion.146
  77.3 45.8 %collective-permute-done.12 = f32[512,2,128]{0,2,1:T(8,128)} collective-permute-done((f32[512,2,128]{0,2,1:T(8,128)}, f32[512,2,128]{0,2,1:T(8,128)}, u32[]{:S(2)}, u32[]{:S(2)}) %collective-permute-start.12) | collective-permute-done | bytes 524320 | tf_op jit(solution)/shard_map/ppermute | solution.py:17
  128.4 2.5 collective-permute-start.17
  131.2 34.8 %collective-permute-done.13 = f32[512,2,128]{2,0,1:T(8,128)} collective-permute-done((f32[512,2,128]{2,0,1:T(8,128)}, f32[512,2,128]{2,0,1:T(8,128)}, u32[]{:S(2)}, u32[]{:S(2)}) %collective-permute-start.13) | collective-permute-done | bytes 524320 | tf_op jit(solution)/shard_map/ppermute | solution.py:17
  171.2 1.9 collective-permute-start.18
  173.3 1.9 collective-permute-start
  175.5 11.8 %collective-permute-done.18 = bf16[512,2,128]{2,0,1:T(8,128)(2,1)S(1)} collective-permute-done((bf16[512,2,128]{2,0,1:T(8,128)(2,1)S(1)}, bf16[512,2,128]{2,0,1:T(8,128)(2,1)S(1)}, u32[]{:S(2)}, u32[]{:S(2)}) %collective-permute-start.18) | collective-permute-done | bytes 262176 | tf_op jit(solution)/shard_map/ppermute | solution.py:17
  188.1 1.9 collective-permute-start.19
  190.0 3.0 collective-permute-done.14
  199.8 3.7 collective-permute-done.19
  205.3 4.6 collective-permute-start.20
  209.9 4.3 collective-permute-done.15
  216.3 3.9 collective-permute-start.16
  220.4 14.1 %collective-permute-done.20 = bf16[512,2,128]{2,0,1:T(8,128)(2,1)S(1)} collective-permute-done((bf16[512,2,128]{2,0,1:T(8,128)(2,1)S(1)}, bf16[512,2,128]{2,0,1:T(8,128)(2,1)S(1)}, u32[]{:S(2)}, u32[]{:S(2)}) %collective-permute-start.20) | collective-permute-done | bytes 262176 | tf_op jit(solution)/shard_map/ppermute | solution.py:17
  235.4 4.1 collective-permute-start.21
  245.7 25.1 %collective-permute-done.21 = bf16[512,2,128]{2,0,1:T(8,128)(2,1)} collective-permute-done((bf16[512,2,128]{2,0,1:T(8,128)(2,1)S(1)}, bf16[512,2,128]{2,0,1:T(8,128)(2,1)}, u32[]{:S(2)}, u32[]{:S(2)}) %collective-permute-start.21) | collective-permute-done | bytes 262176 | tf_op jit(solution)/shard_map/ppermute | solution.py:17
  278.8 2.5 collective-permute-start.27
  283.4 4.1 collective-permute-start.22
  291.3 1.9 collective-permute-start.28
  294.1 38.5 %collective-permute-done.28 = bf16[512,2,128]{2,0,1:T(8,128)(2,1)S(1)} collective-permute-done((bf16[512,2,128]{2,0,1:T(8,128)(2,1)S(1)}, bf16[512,2,128]{2,0,1:T(8,128)(2,1)S(1)}, u32[]{:S(2)}, u32[]{:S(2)}) %collective-permute-start.28) | collective-permute-done | bytes 262176 | tf_op jit(solution)/shard_map/ppermute | solution.py:17
  332.8 4.8 collective-permute-start.29
  340.0 2.1 collective-permute-start.23
  344.4 5.0 collective-permute-done.29
  349.9 15.6 %collective-permute-start.30 = (bf16[512,2,128]{2,0,1:T(8,128)(2,1)S(1)}, bf16[512,2,128]{2,0,1:T(8,128)(2,1)S(1)}, u32[]{:S(2)}, u32[]{:S(2)}) collective-permute-start(bf16[512,2,128]{2,0,1:T(8,128)(2,1)S(1)} %fusion.90), channel_id=1, source_target_pairs={{0,8},{1,9},{2,10},{3,11},{4,12},{5,13},{6,14},{7,15},{8,0},{9,1},... | collective-permute-start | bytes 786440 | tf_op jit(solution)/shard_map/ppermute | solution.py:17
  367.3 41.9 %collective-permute-done.23 = f32[512,2,128]{2,0,1:T(8,128)S(1)} collective-permute-done((f32[512,2,128]{2,0,1:T(8,128)S(1)}, f32[512,2,128]{2,0,1:T(8,128)S(1)}, u32[]{:S(2)}, u32[]{:S(2)}) %collective-permute-start.23) | collective-permute-done | bytes 524320 | tf_op jit(solution)/shard_map/ppermute | solution.py:17
  415.4 8.2 %collective-permute-start.31 = (bf16[512,2,128]{2,0,1:T(8,128)(2,1)S(1)}, bf16[512,2,128]{2,0,1:T(8,128)(2,1)S(1)}, u32[]{:S(2)}, u32[]{:S(2)}) collective-permute-start(bf16[512,2,128]{2,0,1:T(8,128)(2,1)S(1)} %fusion.89), channel_id=1, source_target_pairs={{0,16},{1,17},{2,18},{3,19},{4,20},{5,21},{6,22},{7,23},{8,24},{9,... | collective-permute-start | bytes 786440 | tf_op jit(solution)/shard_map/ppermute | solution.py:17
  424.8 35.1 %collective-permute-done.24 = f32[512,2,128]{2,0,1:T(8,128)S(1)} collective-permute-done((f32[512,2,128]{2,0,1:T(8,128)S(1)}, f32[512,2,128]{2,0,1:T(8,128)S(1)}, u32[]{:S(2)}, u32[]{:S(2)}) %collective-permute-start.24) | collective-permute-done | bytes 524320 | tf_op jit(solution)/shard_map/ppermute | solution.py:17
  464.7 10.5 %collective-permute-done.25 = f32[512,2,128]{2,0,1:T(8,128)S(1)} collective-permute-done((f32[512,2,128]{2,0,1:T(8,128)S(1)}, f32[512,2,128]{2,0,1:T(8,128)S(1)}, u32[]{:S(2)}, u32[]{:S(2)}) %collective-permute-start.25) | collective-permute-done | bytes 524320 | tf_op jit(solution)/shard_map/ppermute | solution.py:17
  475.7 3.4 collective-permute-start.26
  486.8 45.3 %all-reduce = (f32[512]{0:T(512)S(1)}, f32[512]{0:T(512)S(1)}) all-reduce(f32[512]{0:T(512)} %multiply_reduce_fusion.3, f32[512]{0:T(512)} %get-tuple-element.11), channel_id=1, replica_groups=mesh['section'=16,'tp'=32] {'tp'}, use_global_device_ids=true, to_apply=%region_1.0 | all-reduce | flops 1024 | bytes 8192 | tf_op jit(solution)/shard_map/psum | solution.py:60
  534.4 3.4 collective-permute-start.1
  544.3 1.9 collective-permute-start.2
  547.3 6.8 collective-permute-done.2
  557.5 13.5 %collective-permute-done.3 = bf16[512,2,128]{2,0,1:T(8,128)(2,1)S(1)} collective-permute-done((bf16[512,2,128]{2,0,1:T(8,128)(2,1)S(1)}, bf16[512,2,128]{2,0,1:T(8,128)(2,1)S(1)}, u32[]{:S(2)}, u32[]{:S(2)}) %collective-permute-start.3) | collective-permute-done | bytes 262176 | tf_op jit(solution)/shard_map/ppermute | solution.py:17
  571.1 3.2 collective-permute-start.4
  575.4 22.9 %collective-permute-done.4 = bf16[512,2,128]{2,0,1:T(8,128)(2,1)S(1)} collective-permute-done((bf16[512,2,128]{2,0,1:T(8,128)(2,1)S(1)}, bf16[512,2,128]{2,0,1:T(8,128)(2,1)S(1)}, u32[]{:S(2)}, u32[]{:S(2)}) %collective-permute-start.4) | collective-permute-done | bytes 262176 | tf_op jit(solution)/shard_map/ppermute | solution.py:17
  598.5 13.7 %collective-permute-start.5 = (bf16[512,2,128]{2,0,1:T(8,128)(2,1)S(1)}, bf16[512,2,128]{2,0,1:T(8,128)(2,1)S(1)}, u32[]{:S(2)}, u32[]{:S(2)}) collective-permute-start(bf16[512,2,128]{2,0,1:T(8,128)(2,1)S(1)} %fusion.104), channel_id=1, source_target_pairs={{0,16},{1,17},{2,18},{3,19},{4,20},{5,21},{6,22},{7,23},{8,24},{9,... | collective-permute-start | bytes 786440 | tf_op jit(solution)/shard_map/ppermute | solution.py:17
  613.3 16.1 %collective-permute-done.5 = bf16[512,2,128]{2,0,1:T(8,128)(2,1)S(1)} collective-permute-done((bf16[512,2,128]{2,0,1:T(8,128)(2,1)S(1)}, bf16[512,2,128]{2,0,1:T(8,128)(2,1)S(1)}, u32[]{:S(2)}, u32[]{:S(2)}) %collective-permute-start.5) | collective-permute-done | bytes 262176 | tf_op jit(solution)/shard_map/ppermute | solution.py:17
  631.7 2.4 collective-permute-start.6
  638.8 6.8 collective-permute-done.7
  645.8 1.9 collective-permute-start.8
  648.8 13.6 %collective-permute-done.8 = bf16[512,2,128]{2,0,1:T(8,128)(2,1)S(1)} collective-permute-done((bf16[512,2,128]{2,0,1:T(8,128)(2,1)S(1)}, bf16[512,2,128]{2,0,1:T(8,128)(2,1)S(1)}, u32[]{:S(2)}, u32[]{:S(2)}) %collective-permute-start.8) | collective-permute-done | bytes 262176 | tf_op jit(solution)/shard_map/ppermute | solution.py:17
  665.6 24.1 %collective-permute-done.9 = bf16[512,2,128]{2,0,1:T(8,128)(2,1)S(1)} collective-permute-done((bf16[512,2,128]{2,0,1:T(8,128)(2,1)S(1)}, bf16[512,2,128]{2,0,1:T(8,128)(2,1)S(1)}, u32[]{:S(2)}, u32[]{:S(2)}) %collective-permute-start.9) | collective-permute-done | bytes 262176 | tf_op jit(solution)/shard_map/ppermute | solution.py:17
  689.9 7.0 collective-permute-start.10
  699.0 21.2 %collective-permute-done.10 = bf16[512,2,128]{2,0,1:T(8,128)(2,1)S(1)} collective-permute-done((bf16[512,2,128]{2,0,1:T(8,128)(2,1)S(1)}, bf16[512,2,128]{2,0,1:T(8,128)(2,1)S(1)}, u32[]{:S(2)}, u32[]{:S(2)}) %collective-permute-start.10) | collective-permute-done | bytes 262176 | tf_op jit(solution)/shard_map/ppermute | solution.py:17
  (434 shorter events, 106.7 us)
Async XLA Ops:
  0.7 62.8 %copy-start.71 = (bf16[1,2,6,256,128]{4,3,2,1,0:T(8,128)(2,1)S(1)}, bf16[1,2,6,256,128]{4,3,2,1,0:T(8,128)(2,1)}, u32[]{:S(2)}) copy-start(bf16[1,2,6,256,128]{4,3,2,1,0:T(8,128)(2,1)} %param.12) | copy-start | bytes 2359300
  1.8 62.4 %collective-permute-start.11 = (bf16[1,512,256]{1,2,0:T(8,128)(2,1)S(1)}, bf16[1,512,256]{1,2,0:T(8,128)(2,1)S(1)}, u32[]{:S(2)}, u32[]{:S(2)}) collective-permute-start(bf16[1,512,256]{1,2,0:T(8,128)(2,1)S(1)} %copy.52), channel_id=1, source_target_pairs={{0,480},{32,0},{64,32},{96,64},{128,96},{160,128},{192,160},{224,1... | collective-permute-start | bytes 786440 | tf_op jit(solution)/shard_map/ppermute | solution.py:23
  10.7 53.5 %copy-start.128 = (f32[2]{0:T(128)}, f32[2]{0:T(128)S(1)}, u32[]{:S(2)}) copy-start(f32[2]{0:T(128)S(1)} %get-tuple-element.12) | copy-start | bytes 28
  64.2 63.4 %copy-start.32 = (bf16[1,1,1,256,128]{4,3,2,1,0:T(8,128)(2,1)}, bf16[1,1,1,256,128]{4,3,2,1,0:T(8,128)(2,1)S(1)}, u32[]{:S(2)}) copy-start(bf16[1,1,1,256,128]{4,3,2,1,0:T(8,128)(2,1)S(1)} %get-tuple-element.35) | copy-start | bytes 196612
  64.2 106.1 %copy-start.29 = (bf16[1,1,1,256,128]{4,3,2,1,0:T(8,128)(2,1)}, bf16[1,1,1,256,128]{4,3,2,1,0:T(8,128)(2,1)S(1)}, u32[]{:S(2)}) copy-start(bf16[1,1,1,256,128]{4,3,2,1,0:T(8,128)(2,1)S(1)} %get-tuple-element.34) | copy-start | bytes 196612
  64.2 123.1 %copy-start.26 = (bf16[1,1,1,256,128]{4,3,2,1,0:T(8,128)(2,1)}, bf16[1,1,1,256,128]{4,3,2,1,0:T(8,128)(2,1)S(1)}, u32[]{:S(2)}) copy-start(bf16[1,1,1,256,128]{4,3,2,1,0:T(8,128)(2,1)S(1)} %get-tuple-element.33) | copy-start | bytes 196612
  64.2 130.1 %copy-start.15 = (bf16[1,1,1,256,128]{4,3,2,1,0:T(8,128)(2,1)}, bf16[1,1,1,256,128]{4,3,2,1,0:T(8,128)(2,1)S(1)}, u32[]{:S(2)}) copy-start(bf16[1,1,1,256,128]{4,3,2,1,0:T(8,128)(2,1)S(1)} %get-tuple-element.28) | copy-start | bytes 196612
  64.2 139.3 %copy-start.24 = (bf16[1,1,1,256,128]{4,3,2,1,0:T(8,128)(2,1)}, bf16[1,1,1,256,128]{4,3,2,1,0:T(8,128)(2,1)S(1)}, u32[]{:S(2)}) copy-start(bf16[1,1,1,256,128]{4,3,2,1,0:T(8,128)(2,1)S(1)} %get-tuple-element.32) | copy-start | bytes 196612
  64.2 151.3 %copy-start.17 = (bf16[1,1,1,256,128]{4,3,2,1,0:T(8,128)(2,1)}, bf16[1,1,1,256,128]{4,3,2,1,0:T(8,128)(2,1)S(1)}, u32[]{:S(2)}) copy-start(bf16[1,1,1,256,128]{4,3,2,1,0:T(8,128)(2,1)S(1)} %get-tuple-element.29) | copy-start | bytes 196612
  64.2 170.3 %copy-start.22 = (bf16[1,1,1,256,128]{4,3,2,1,0:T(8,128)(2,1)}, bf16[1,1,1,256,128]{4,3,2,1,0:T(8,128)(2,1)S(1)}, u32[]{:S(2)}) copy-start(bf16[1,1,1,256,128]{4,3,2,1,0:T(8,128)(2,1)S(1)} %get-tuple-element.31) | copy-start | bytes 196612
  65.2 57.9 %collective-permute-start.12 = (f32[512,2,128]{0,2,1:T(8,128)}, f32[512,2,128]{0,2,1:T(8,128)}, u32[]{:S(2)}, u32[]{:S(2)}) collective-permute-start(f32[512,2,128]{0,2,1:T(8,128)} %fusion.34), channel_id=1, source_target_pairs={{0,16},{1,17},{2,18},{3,19},{4,20},{5,21},{6,22},{7,23},{8,24},{9,... | collective-permute-start | bytes 1572872 | tf_op jit(solution)/shard_map/ppermute | solution.py:17
  76.3 46.8 %copy-start.74 = (bf16[1,1,1,256,128]{4,3,2,1,0:T(8,128)(2,1)}, bf16[1,1,1,256,128]{4,3,2,1,0:T(8,128)(2,1)S(1)}, u32[]{:S(2)}) copy-start(bf16[1,1,1,256,128]{4,3,2,1,0:T(8,128)(2,1)S(1)} %get-tuple-element.48) | copy-start | bytes 196612
  76.3 54.7 %copy-start.67 = (bf16[1,1,1,256,128]{4,3,2,1,0:T(8,128)(2,1)}, bf16[1,1,1,256,128]{4,3,2,1,0:T(8,128)(2,1)S(1)}, u32[]{:S(2)}) copy-start(bf16[1,1,1,256,128]{4,3,2,1,0:T(8,128)(2,1)S(1)} %get-tuple-element.46) | copy-start | bytes 196612
  76.3 89.7 %copy-start.43 = (bf16[1,1,1,256,128]{4,3,2,1,0:T(8,128)(2,1)}, bf16[1,1,1,256,128]{4,3,2,1,0:T(8,128)(2,1)S(1)}, u32[]{:S(2)}) copy-start(bf16[1,1,1,256,128]{4,3,2,1,0:T(8,128)(2,1)S(1)} %get-tuple-element.49) | copy-start | bytes 196612
  76.3 98.9 %copy-start.64 = (bf16[1,1,1,256,128]{4,3,2,1,0:T(8,128)(2,1)}, bf16[1,1,1,256,128]{4,3,2,1,0:T(8,128)(2,1)S(1)}, u32[]{:S(2)}) copy-start(bf16[1,1,1,256,128]{4,3,2,1,0:T(8,128)(2,1)S(1)} %get-tuple-element.45) | copy-start | bytes 196612
  125.5 40.5 %collective-permute-start.13 = (f32[512,2,128]{2,0,1:T(8,128)}, f32[512,2,128]{2,0,1:T(8,128)}, u32[]{:S(2)}, u32[]{:S(2)}) collective-permute-start(f32[512,2,128]{2,0,1:T(8,128)} %fusion.33), channel_id=1, source_target_pairs={{0,8},{1,9},{2,10},{3,11},{4,12},{5,13},{6,14},{7,15},{8,0},{9,1},... | collective-permute-start | bytes 1572872 | tf_op jit(solution)/shard_map/ppermute | solution.py:17
  128.4 41.9 %collective-permute-start.17 = (bf16[512,2,128]{2,0,1:T(8,128)(2,1)S(1)}, bf16[512,2,128]{2,0,1:T(8,128)(2,1)S(1)}, u32[]{:S(2)}, u32[]{:S(2)}) collective-permute-start(bf16[512,2,128]{2,0,1:T(8,128)(2,1)S(1)} %fusion.98), channel_id=1, source_target_pairs={{0,1},{1,0},{2,3},{3,2},{4,5},{5,4},{6,7},{7,6},{8,9},{9,8},{10,11... | collective-permute-start | bytes 786440 | tf_op jit(solution)/shard_map/ppermute | solution.py:17
  168.4 24.7 %collective-permute-start.14 = (f32[512,2,128]{2,0,1:T(8,128)}, f32[512,2,128]{2,0,1:T(8,128)}, u32[]{:S(2)}, u32[]{:S(2)}) collective-permute-start(f32[512,2,128]{2,0,1:T(8,128)} %fusion.32), channel_id=1, source_target_pairs={{0,4},{1,5},{2,6},{3,7},{4,0},{5,1},{6,2},{7,3},{8,12},{9,13},{10,... | collective-permute-start | bytes 1572872 | tf_op jit(solution)/shard_map/ppermute | solution.py:17
  171.2 16.0 %collective-permute-start.18 = (bf16[512,2,128]{2,0,1:T(8,128)(2,1)S(1)}, bf16[512,2,128]{2,0,1:T(8,128)(2,1)S(1)}, u32[]{:S(2)}, u32[]{:S(2)}) collective-permute-start(bf16[512,2,128]{2,0,1:T(8,128)(2,1)S(1)} %fusion.97), channel_id=1, source_target_pairs={{0,2},{1,3},{2,0},{3,1},{4,6},{5,7},{6,4},{7,5},{8,10},{9,11},{10,... | collective-permute-start | bytes 786440 | tf_op jit(solution)/shard_map/ppermute | solution.py:17
  173.3 24.6 %collective-permute-start = (bf16[1,512,256]{1,2,0:T(8,128)(2,1)S(1)}, bf16[1,512,256]{1,2,0:T(8,128)(2,1)S(1)}, u32[]{:S(2)}, u32[]{:S(2)}) collective-permute-start(bf16[1,512,256]{1,2,0:T(8,128)(2,1)S(1)} %copy.47), channel_id=1, source_target_pairs={{0,32},{32,64},{64,96},{96,128},{128,160},{160,192},{192,224},{224... | collective-permute-start | bytes 786440 | tf_op jit(solution)/shard_map/ppermute | solution.py:23
  188.1 15.3 %collective-permute-start.19 = (bf16[512,2,128]{2,0,1:T(8,128)(2,1)S(1)}, bf16[512,2,128]{2,0,1:T(8,128)(2,1)}, u32[]{:S(2)}, u32[]{:S(2)}) collective-permute-start(bf16[512,2,128]{2,0,1:T(8,128)(2,1)S(1)} %fusion.96), channel_id=1, source_target_pairs={{0,4},{1,5},{2,6},{3,7},{4,0},{5,1},{6,2},{7,3},{8,12},{9,13},{10,... | collective-permute-start | bytes 786440 | tf_op jit(solution)/shard_map/ppermute | solution.py:17
  195.9 18.3 %collective-permute-start.15 = (f32[512,2,128]{2,0,1:T(8,128)}, f32[512,2,128]{2,0,1:T(8,128)}, u32[]{:S(2)}, u32[]{:S(2)}) collective-permute-start(f32[512,2,128]{2,0,1:T(8,128)} %fusion.31), channel_id=1, source_target_pairs={{0,2},{1,3},{2,0},{3,1},{4,6},{5,7},{6,4},{7,5},{8,10},{9,11},{10,... | collective-permute-start | bytes 1572872 | tf_op jit(solution)/shard_map/ppermute | solution.py:17
  205.3 29.2 %collective-permute-start.20 = (bf16[512,2,128]{2,0,1:T(8,128)(2,1)S(1)}, bf16[512,2,128]{2,0,1:T(8,128)(2,1)S(1)}, u32[]{:S(2)}, u32[]{:S(2)}) collective-permute-start(bf16[512,2,128]{2,0,1:T(8,128)(2,1)S(1)} %fusion.95), channel_id=1, source_target_pairs={{0,8},{1,9},{2,10},{3,11},{4,12},{5,13},{6,14},{7,15},{8,0},{9,1},... | collective-permute-start | bytes 786440 | tf_op jit(solution)/shard_map/ppermute | solution.py:17
  216.3 24.2 %collective-permute-start.16 = (f32[512,2,128]{2,0,1:T(8,128)S(1)}, f32[512,2,128]{2,0,1:T(8,128)S(1)}, u32[]{:S(2)}, u32[]{:S(2)}) collective-permute-start(f32[512,2,128]{2,0,1:T(8,128)S(1)} %fusion.30), channel_id=1, source_target_pairs={{0,1},{1,0},{2,3},{3,2},{4,5},{5,4},{6,7},{7,6},{8,9},{9,8},{10,11... | collective-permute-start | bytes 1572872 | tf_op jit(solution)/shard_map/ppermute | solution.py:17
  235.4 35.4 %collective-permute-start.21 = (bf16[512,2,128]{2,0,1:T(8,128)(2,1)S(1)}, bf16[512,2,128]{2,0,1:T(8,128)(2,1)}, u32[]{:S(2)}, u32[]{:S(2)}) collective-permute-start(bf16[512,2,128]{2,0,1:T(8,128)(2,1)S(1)} %fusion.94), channel_id=1, source_target_pairs={{0,16},{1,17},{2,18},{3,19},{4,20},{5,21},{6,22},{7,23},{8,24},{9,... | collective-permute-start | bytes 786440 | tf_op jit(solution)/shard_map/ppermute | solution.py:17
  278.8 11.6 %collective-permute-start.27 = (bf16[512,2,128]{2,0,1:T(8,128)(2,1)S(1)}, bf16[512,2,128]{2,0,1:T(8,128)(2,1)S(1)}, u32[]{:S(2)}, u32[]{:S(2)}) collective-permute-start(bf16[512,2,128]{2,0,1:T(8,128)(2,1)S(1)} %fusion.93), channel_id=1, source_target_pairs={{0,1},{1,0},{2,3},{3,2},{4,5},{5,4},{6,7},{7,6},{8,9},{9,8},{10,11... | collective-permute-start | bytes 786440 | tf_op jit(solution)/shard_map/ppermute | solution.py:17
  283.4 54.6 %collective-permute-start.22 = (f32[512,2,128]{2,0,1:T(8,128)S(1)}, f32[512,2,128]{2,0,1:T(8,128)S(1)}, u32[]{:S(2)}, u32[]{:S(2)}) collective-permute-start(f32[512,2,128]{2,0,1:T(8,128)S(1)} %fusion.22), channel_id=1, source_target_pairs={{0,16},{1,17},{2,18},{3,19},{4,20},{5,21},{6,22},{7,23},{8,24},{9,... | collective-permute-start | bytes 1572872 | tf_op jit(solution)/shard_map/ppermute | solution.py:17
  291.3 41.3 %collective-permute-start.28 = (bf16[512,2,128]{2,0,1:T(8,128)(2,1)S(1)}, bf16[512,2,128]{2,0,1:T(8,128)(2,1)S(1)}, u32[]{:S(2)}, u32[]{:S(2)}) collective-permute-start(bf16[512,2,128]{2,0,1:T(8,128)(2,1)S(1)} %fusion.92), channel_id=1, source_target_pairs={{0,2},{1,3},{2,0},{3,1},{4,6},{5,7},{6,4},{7,5},{8,10},{9,11},{10,... | collective-permute-start | bytes 786440 | tf_op jit(solution)/shard_map/ppermute | solution.py:17
  332.8 16.6 %collective-permute-start.29 = (bf16[512,2,128]{2,0,1:T(8,128)(2,1)S(1)}, bf16[512,2,128]{2,0,1:T(8,128)(2,1)S(1)}, u32[]{:S(2)}, u32[]{:S(2)}) collective-permute-start(bf16[512,2,128]{2,0,1:T(8,128)(2,1)S(1)} %fusion.91), channel_id=1, source_target_pairs={{0,4},{1,5},{2,6},{3,7},{4,0},{5,1},{6,2},{7,3},{8,12},{9,13},{10,... | collective-permute-start | bytes 786440 | tf_op jit(solution)/shard_map/ppermute | solution.py:17
  340.0 69.2 %collective-permute-start.23 = (f32[512,2,128]{2,0,1:T(8,128)S(1)}, f32[512,2,128]{2,0,1:T(8,128)S(1)}, u32[]{:S(2)}, u32[]{:S(2)}) collective-permute-start(f32[512,2,128]{2,0,1:T(8,128)S(1)} %fusion.21), channel_id=1, source_target_pairs={{0,8},{1,9},{2,10},{3,11},{4,12},{5,13},{6,14},{7,15},{8,0},{9,1},... | collective-permute-start | bytes 1572872 | tf_op jit(solution)/shard_map/ppermute | solution.py:17
  349.9 65.3 %collective-permute-start.30 = (bf16[512,2,128]{2,0,1:T(8,128)(2,1)S(1)}, bf16[512,2,128]{2,0,1:T(8,128)(2,1)S(1)}, u32[]{:S(2)}, u32[]{:S(2)}) collective-permute-start(bf16[512,2,128]{2,0,1:T(8,128)(2,1)S(1)} %fusion.90), channel_id=1, source_target_pairs={{0,8},{1,9},{2,10},{3,11},{4,12},{5,13},{6,14},{7,15},{8,0},{9,1},... | collective-permute-start | bytes 786440 | tf_op jit(solution)/shard_map/ppermute | solution.py:17
  366.6 42.7 %copy-start.59 = (bf16[1,1,1,256,128]{4,3,2,1,0:T(8,128)(2,1)S(1)}, bf16[1,1,1,256,128]{4,3,2,1,0:T(8,128)(2,1)}, u32[]{:S(2)}) copy-start(bf16[1,1,1,256,128]{4,3,2,1,0:T(8,128)(2,1)} %get-tuple-element.43) | copy-start | bytes 196612
  367.3 42.2 %copy-start.117 = (f32[2]{0:T(128)S(1)}, f32[2]{0:T(128)}, u32[]{:S(2)}) copy-start(f32[2]{0:T(128)} %get-tuple-element.20) | copy-start | bytes 28
  411.4 48.4 %collective-permute-start.24 = (f32[512,2,128]{2,0,1:T(8,128)S(1)}, f32[512,2,128]{2,0,1:T(8,128)S(1)}, u32[]{:S(2)}, u32[]{:S(2)}) collective-permute-start(f32[512,2,128]{2,0,1:T(8,128)S(1)} %fusion.20), channel_id=1, source_target_pairs={{0,4},{1,5},{2,6},{3,7},{4,0},{5,1},{6,2},{7,3},{8,12},{9,13},{10,... | collective-permute-start | bytes 1572872 | tf_op jit(solution)/shard_map/ppermute | solution.py:17
  415.4 46.9 %collective-permute-start.31 = (bf16[512,2,128]{2,0,1:T(8,128)(2,1)S(1)}, bf16[512,2,128]{2,0,1:T(8,128)(2,1)S(1)}, u32[]{:S(2)}, u32[]{:S(2)}) collective-permute-start(bf16[512,2,128]{2,0,1:T(8,128)(2,1)S(1)} %fusion.89), channel_id=1, source_target_pairs={{0,16},{1,17},{2,18},{3,19},{4,20},{5,21},{6,22},{7,23},{8,24},{9,... | collective-permute-start | bytes 786440 | tf_op jit(solution)/shard_map/ppermute | solution.py:17
  460.3 14.9 %collective-permute-start.25 = (f32[512,2,128]{2,0,1:T(8,128)S(1)}, f32[512,2,128]{2,0,1:T(8,128)S(1)}, u32[]{:S(2)}, u32[]{:S(2)}) collective-permute-start(f32[512,2,128]{2,0,1:T(8,128)S(1)} %fusion.19), channel_id=1, source_target_pairs={{0,2},{1,3},{2,0},{3,1},{4,6},{5,7},{6,4},{7,5},{8,10},{9,11},{10,... | collective-permute-start | bytes 1572872 | tf_op jit(solution)/shard_map/ppermute | solution.py:17
  475.7 6.2 collective-permute-start.26
  486.8 45.4 %copy-start.14 = (f32[512,2,128]{2,0,1:T(8,128)S(1)}, f32[512,2,128]{2,0,1:T(8,128)}, u32[]{:S(2)}) copy-start(f32[512,2,128]{2,0,1:T(8,128)} %copy.48) | copy-start | bytes 1572868
  534.4 8.2 %collective-permute-start.1 = (bf16[512,2,128]{2,0,1:T(8,128)(2,1)S(1)}, bf16[512,2,128]{2,0,1:T(8,128)(2,1)}, u32[]{:S(2)}, u32[]{:S(2)}) collective-permute-start(bf16[512,2,128]{2,0,1:T(8,128)(2,1)S(1)} %fusion.108), channel_id=1, source_target_pairs={{0,1},{1,0},{2,3},{3,2},{4,5},{5,4},{6,7},{7,6},{8,9},{9,8},{10,11... | collective-permute-start | bytes 786440 | tf_op jit(solution)/shard_map/ppermute | solution.py:17
  544.3 9.8 %collective-permute-start.2 = (bf16[512,2,128]{2,0,1:T(8,128)(2,1)S(1)}, bf16[512,2,128]{2,0,1:T(8,128)(2,1)S(1)}, u32[]{:S(2)}, u32[]{:S(2)}) collective-permute-start(bf16[512,2,128]{2,0,1:T(8,128)(2,1)S(1)} %fusion.107), channel_id=1, source_target_pairs={{0,2},{1,3},{2,0},{3,1},{4,6},{5,7},{6,4},{7,5},{8,10},{9,11},{10,... | collective-permute-start | bytes 786440 | tf_op jit(solution)/shard_map/ppermute | solution.py:17
  554.3 16.6 %collective-permute-start.3 = (bf16[512,2,128]{2,0,1:T(8,128)(2,1)S(1)}, bf16[512,2,128]{2,0,1:T(8,128)(2,1)S(1)}, u32[]{:S(2)}, u32[]{:S(2)}) collective-permute-start(bf16[512,2,128]{2,0,1:T(8,128)(2,1)S(1)} %fusion.106), channel_id=1, source_target_pairs={{0,4},{1,5},{2,6},{3,7},{4,0},{5,1},{6,2},{7,3},{8,12},{9,13},{10,... | collective-permute-start | bytes 786440 | tf_op jit(solution)/shard_map/ppermute | solution.py:17
  571.1 27.2 %collective-permute-start.4 = (bf16[512,2,128]{2,0,1:T(8,128)(2,1)S(1)}, bf16[512,2,128]{2,0,1:T(8,128)(2,1)S(1)}, u32[]{:S(2)}, u32[]{:S(2)}) collective-permute-start(bf16[512,2,128]{2,0,1:T(8,128)(2,1)S(1)} %fusion.105), channel_id=1, source_target_pairs={{0,8},{1,9},{2,10},{3,11},{4,12},{5,13},{6,14},{7,15},{8,0},{9,1},... | collective-permute-start | bytes 786440 | tf_op jit(solution)/shard_map/ppermute | solution.py:17
  598.5 30.9 %collective-permute-start.5 = (bf16[512,2,128]{2,0,1:T(8,128)(2,1)S(1)}, bf16[512,2,128]{2,0,1:T(8,128)(2,1)S(1)}, u32[]{:S(2)}, u32[]{:S(2)}) collective-permute-start(bf16[512,2,128]{2,0,1:T(8,128)(2,1)S(1)} %fusion.104), channel_id=1, source_target_pairs={{0,16},{1,17},{2,18},{3,19},{4,20},{5,21},{6,22},{7,23},{8,24},{9,... | collective-permute-start | bytes 786440 | tf_op jit(solution)/shard_map/ppermute | solution.py:17
  631.7 3.6 collective-permute-start.6
  635.8 9.8 %collective-permute-start.7 = (bf16[512,2,128]{2,0,1:T(8,128)(2,1)S(1)}, bf16[512,2,128]{2,0,1:T(8,128)(2,1)S(1)}, u32[]{:S(2)}, u32[]{:S(2)}) collective-permute-start(bf16[512,2,128]{2,0,1:T(8,128)(2,1)S(1)} %fusion.102), channel_id=1, source_target_pairs={{0,2},{1,3},{2,0},{3,1},{4,6},{5,7},{6,4},{7,5},{8,10},{9,11},{10,... | collective-permute-start | bytes 786440 | tf_op jit(solution)/shard_map/ppermute | solution.py:17
  645.8 16.6 %collective-permute-start.8 = (bf16[512,2,128]{2,0,1:T(8,128)(2,1)S(1)}, bf16[512,2,128]{2,0,1:T(8,128)(2,1)S(1)}, u32[]{:S(2)}, u32[]{:S(2)}) collective-permute-start(bf16[512,2,128]{2,0,1:T(8,128)(2,1)S(1)} %fusion.101), channel_id=1, source_target_pairs={{0,4},{1,5},{2,6},{3,7},{4,0},{5,1},{6,2},{7,3},{8,12},{9,13},{10,... | collective-permute-start | bytes 786440 | tf_op jit(solution)/shard_map/ppermute | solution.py:17
  662.6 27.1 %collective-permute-start.9 = (bf16[512,2,128]{2,0,1:T(8,128)(2,1)S(1)}, bf16[512,2,128]{2,0,1:T(8,128)(2,1)S(1)}, u32[]{:S(2)}, u32[]{:S(2)}) collective-permute-start(bf16[512,2,128]{2,0,1:T(8,128)(2,1)S(1)} %fusion.100), channel_id=1, source_target_pairs={{0,8},{1,9},{2,10},{3,11},{4,12},{5,13},{6,14},{7,15},{8,0},{9,1},... | collective-permute-start | bytes 786440 | tf_op jit(solution)/shard_map/ppermute | solution.py:17
  689.9 30.2 %collective-permute-start.10 = (bf16[512,2,128]{2,0,1:T(8,128)(2,1)S(1)}, bf16[512,2,128]{2,0,1:T(8,128)(2,1)S(1)}, u32[]{:S(2)}, u32[]{:S(2)}) collective-permute-start(bf16[512,2,128]{2,0,1:T(8,128)(2,1)S(1)} %fusion.99), channel_id=1, source_target_pairs={{0,16},{1,17},{2,18},{3,19},{4,20},{5,21},{6,22},{7,23},{8,24},{9,... | collective-permute-start | bytes 786440 | tf_op jit(solution)/shard_map/ppermute | solution.py:17
  (119 other events, 743.6 us)
where the time goes:
time: 725 us; the launch traced here: 721 us
  waiting for transfers between devices  399 us (55%)
  starting transfers between devices  129 us (18%)
  blocking collectives  98 us (14%)
  matrix products  49.5 us (7%)
  local copies, waits for them, and re-layouts  40.6 us (6%)
    ppermute x30, waiting for transfers between devices, from_partner(): return lax.ppermute(value, axis, pairs)  399 us
    ppermute x30, starting transfers between devices, from_partner(): return lax.ppermute(value, axis, pairs)  119 us
    psum x2, blocking collectives, normalize(): squares = lax.psum(jnp.sum(values * values, axis=1), 'tp')  98 us
    unnamed x295, local copies, waits for them, and re-layouts  31.9 us
    dot_general x24, matrix products, block_grad(): jnp.einsum('tlc,tld->lcd', values, grads, preferred_element_type=jnp.floa...  18 us
    dot_general x24, matrix products, block_back(): jnp.einsum('tld,lcd->tlc', grads, weights, preferred_element_type=jnp.flo...  16.4 us
    dot_general x46, matrix products, block_mix(): jnp.einsum('tlc,lcd->tld', values, weights, preferred_element_type=jnp.fl...  15.1 us
  transfers between devices with their start and end apart: 32, of which 22 were waited for; matrix products, arithmetic and copies ran while one was open for 6% of the time, Pallas kernels for 0%

commit v1 on v0

v1 whole, which is shorter than its diff:
```python
import jax
import jax.numpy as jnp
from jax import lax
from jax.sharding import PartitionSpec as P

D = 8192


EPSILON = 1e-05
GELU_C = 0.7978845608028654
GELU_A = 0.044715


def from_partner(value, axis, apart):
    mask = 2**apart
    pairs = [(source, source ^ mask) for source in range(lax.axis_size(axis))]
    return lax.ppermute(value, axis, pairs)


def from_behind(value, axis, steps):
    count = lax.axis_size(axis)
    pairs = [(source, (source + steps) % count) for source in range(count)]
    return lax.ppermute(value, axis, pairs)


def gelu_value(v):
    inner = GELU_C * (v + GELU_A * v * v * v)
    return 0.5 * v * (1.0 + jnp.tanh(inner))


def gelu_slope(v):
    inner = GELU_C * (v + GELU_A * v * v * v)
    tanh_val = jnp.tanh(inner)
    return 0.5 * (1.0 + tanh_val) + 0.5 * v * (1.0 - tanh_val * tanh_val) * GELU_C * (
        1.0 + 3.0 * GELU_A * v * v
    )


def flip_blocks(x, k, axis):
    shape = x.shape
    low = 2**k
    parts = shape[:axis] + (shape[axis] // (2 * low), 2, low) + shape[axis + 1 :]
    return jnp.flip(x.reshape(parts), axis + 1).reshape(shape)


def block_mix(values, weights):
    return jnp.einsum("tlc,lcd->tld", values, weights, preferred_element_type=jnp.float32)


def block_back(grads, weights):
    return jnp.einsum("tld,lcd->tlc", grads, weights, preferred_element_type=jnp.float32)


def block_grad(values, grads):
    return jnp.einsum("tlc,tld->lcd", values, grads, preferred_element_type=jnp.float32)


def sum_squares(x):
    values = x.astype(jnp.float32)
    return lax.psum(jnp.sum(values * values, axis=1), "tp")


def factor_forward(values, selfw, partw, mask, k, local_bits, finish):
    if k < local_bits:
        other = flip_blocks(values, k, 1)
    else:
        other = from_partner(values, "tp", k - local_bits)
    if not finish:
        return None, other
    mixed = block_mix(values, selfw[k]) + mask[k][None, :, None] * block_mix(other, partw[k])
    return mixed.astype(jnp.bfloat16), other


def factor_backward(grads, selfw, partw, mask, k, local_bits):
    term = (mask[k][None, :, None] * block_back(grads, partw[k])).astype(jnp.bfloat16)
    if k < local_bits:
        back = flip_blocks(term, k, 1)
    else:
        back = from_partner(term, "tp", k - local_bits)
    own = block_back(grads, selfw[k])
    return (own + back.astype(jnp.float32)).astype(jnp.bfloat16)


def weight_grads(inputs, partners, cots, mask):
    grads_self = jnp.stack([block_grad(v, g).astype(jnp.bfloat16) for v, g in zip(inputs, cots)])
    grads_part = jnp.stack(
        [
            (mask[k][:, None, None] * block_grad(v, g)).astype(jnp.bfloat16)
            for k, (v, g) in enumerate(zip(partners, cots))
        ]
    )
    return grads_self, grads_part


def per_device(sent_act, stash, grad_back, gain, self_blocks, partner_blocks, block_mask):
    tokens = sent_act.shape[1]
    width = sent_act.shape[2]
    block = self_blocks.shape[4]
    factors = self_blocks.shape[2]
    local_blocks = width // block
    local_bits = local_blocks.bit_length() - 1
    selfw = self_blocks[0].reshape(2, factors, local_blocks, block, block)
    partw = partner_blocks[0].reshape(2, factors, local_blocks, block, block)
    mask = block_mask[0].astype(jnp.float32)
    gain_row = gain[0]
    wide = (tokens, local_blocks, block)
    returning = from_behind(grad_back, "section", -1)[0]
    arriving = from_behind(sent_act, "section", 1)[0]
    held = stash[0]
    scale_s = lax.rsqrt(sum_squares(held) / D + EPSILON)[:, None, None]
    scale_a = lax.rsqrt(sum_squares(arriving) / D + EPSILON)[:, None, None]
    s = (held.astype(jnp.float32) * gain_row[None, :]).astype(jnp.bfloat16).reshape(wide)
    a = (arriving.astype(jnp.float32) * gain_row[None, :]).astype(jnp.bfloat16).reshape(wide)
    b = returning.reshape(wide)
    s_in, s_par, b_cot = [[], []], [[], []], [[None] * factors, [None] * factors]
    for p in range(2):
        for k in range(factors):
            r = factors - 1 - k
            b_cot[1 - p][r] = b
            s_in[p].append(s)
            b_next = factor_backward(b, selfw[1 - p], partw[1 - p], mask[1 - p], r, local_bits)
            s_next, other = factor_forward(
                s, selfw[p], partw[p], mask[p], k, local_bits, p == 0 or k + 1 < factors
            )
            s_par[p].append(other)
            a, _ = factor_forward(a, selfw[p], partw[p], mask[p], k, local_bits, True)
            s, b = s_next, b_next
        if p == 0:
            pre_s = s.astype(jnp.float32) * scale_s
            s = gelu_value(pre_s).astype(jnp.bfloat16)
            a = gelu_value(a.astype(jnp.float32) * scale_a).astype(jnp.bfloat16)
            da = b.astype(jnp.float32) * gelu_slope(pre_s)
            corr = lax.psum(jnp.sum(da * pre_s, axis=(1, 2)), "tp")
            b = (da * scale_s).astype(jnp.bfloat16)
    out_act = (arriving.astype(jnp.float32) + a.reshape(tokens, width).astype(jnp.float32)).astype(
        jnp.bfloat16
    )
    gs_first, gp_first = weight_grads(s_in[0], s_par[0], b_cot[0], mask[0])
    gs_second, gp_second = weight_grads(s_in[1], s_par[1], b_cot[1], mask[1])
    du = b.reshape(tokens, width).astype(jnp.float32)
    xs = held.astype(jnp.float32)
    grad_gain = jnp.sum(du * xs, axis=0)
    back = (scale_s[:, 0, 0] * scale_s[:, 0, 0] * corr / D)[:, None]
    grad_in = (returning.astype(jnp.float32) + (du * gain_row[None, :] - xs * back)).astype(
        jnp.bfloat16
    )
    grad_self = jnp.stack([gs_first, gs_second]).reshape(1, 2, factors, width, block)
    grad_partner = jnp.stack([gp_first, gp_second]).reshape(1, 2, factors, width, block)
    return (out_act[None], grad_in[None], grad_self, grad_partner, grad_gain[None])


def solution(mesh):
    in_specs = (
        P("section", None, "tp"),
        P("section", None, "tp"),
        P("section", None, "tp"),
        P("section", "tp"),
        P("section", None, None, "tp", None),
        P("section", None, None, "tp", None),
        P("section", None, None, "tp"),
    )
    out_specs = (
        P("section", None, "tp"),
        P("section", None, "tp"),
        P("section", None, None, "tp", None),
        P("section", None, None, "tp", None),
        P("section", "tp"),
    )
    return jax.shard_map(
        per_device, mesh=mesh, in_specs=in_specs, out_specs=out_specs, check_vma=False
    )
```

time: 725 us -> 560 us (0.77)
  waiting for transfers between devices: 399 us -> 249 us
  starting transfers between devices: 129 us -> 112 us
    ppermute x30, waiting for transfers between devices: 399 us -> 249 us  [from_partner(): return lax.ppermute(value, axis, pairs)]
    ppermute x30, starting transfers between devices: 119 us -> 103 us  [from_partner(): return lax.ppermute(value, axis, pairs)]
    dot_general x46, matrix products: 15.1 us -> 25.3 us  [block_mix(): jnp.einsum('tlc,lcd->tld', values, weights, preferred_element_type=jnp.fl...]
    dot_general x24, matrix products: 16.4 us -> 8.55 us  [block_back(): jnp.einsum('tld,lcd->tlc', grads, weights, preferred_element_type=jnp.flo...]
    unnamed x295 -> x269, local copies, waits for them, and re-layouts: 31.9 us -> 31.1 us
  transfers between devices with their start and end apart: 32 -> 32, of which waited for: 22 -> 13; matrix products, arithmetic and copies ran while one was open for 6% -> 10% of each run, Pallas kernels for 0% -> 0%
where the time goes in v1:
time: 560 us; the launch traced here: 558 us
  waiting for transfers between devices  249 us (44%)
  starting transfers between devices  112 us (20%)
  blocking collectives  100 us (18%)
  matrix products  49 us (9%)
  local copies, waits for them, and re-layouts  39 us (7%)
  other arithmetic  5.68 us (1%)
    ppermute x30, waiting for transfers between devices, from_partner(): return lax.ppermute(value, axis, pairs)  249 us
    ppermute x30, starting transfers between devices, from_partner(): return lax.ppermute(value, axis, pairs)  103 us
    psum x2, blocking collectives, sum_squares(): return lax.psum(jnp.sum(values * values, axis=1), 'tp')  100 us
    unnamed x269, local copies, waits for them, and re-layouts  31.1 us
    dot_general x46, matrix products, block_mix(): jnp.einsum('tlc,lcd->tld', values, weights, preferred_element_type=jnp.fl...  25.3 us
    dot_general x24, matrix products, block_grad(): jnp.einsum('tlc,tld->lcd', values, grads, preferred_element_type=jnp.floa...  15.2 us
  transfers between devices with their start and end apart: 32, of which 13 were waited for; matrix products, arithmetic and copies ran while one was open for 10% of the time, Pallas kernels for 0%

profile of v1, /device:TPU:1, one launch (start us, length us, event | category | flops | bytes accessed | tf_op | source)
XLA Modules:
  0.0 557.7 jit_solution(3736701921665991039)
XLA Ops:
  2.5 4.0 collective-permute-start
  7.4 5.7 %collective-permute-start.11 = (bf16[1,512,256]{1,2,0:T(8,128)(2,1)}, bf16[1,512,256]{1,2,0:T(8,128)(2,1)S(1)}, u32[]{:S(2)}, u32[]{:S(2)}) collective-permute-start(bf16[1,512,256]{1,2,0:T(8,128)(2,1)} %copy.57), channel_id=1, source_target_pairs={{0,480},{32,0},{64,32},{96,64},{128,96},{160,128},{192,160},{224,1... | collective-permute-start | bytes 786440 | tf_op jit(solution)/shard_map/ppermute | solution.py:23
  15.6 52.9 %psum.22 = f32[512]{0:T(512)S(1)} all-reduce(f32[512]{0:T(512)S(1)} %multiply_reduce_fusion.2), channel_id=1, replica_groups=mesh['section'=16,'tp'=32] {'tp'}, use_global_device_ids=true, to_apply=%region_3.0 | all-reduce | flops 512 | bytes 4096 | tf_op jit(solution)/shard_map/psum | solution.py:60
  73.7 4.4 collective-permute-start.1
  78.5 1.9 collective-permute-start.17
  81.5 6.9 %collective-permute-start.12 = (bf16[512,2,128]{0,2,1:T(8,128)(2,1)S(1)}, bf16[512,2,128]{0,2,1:T(8,128)(2,1)S(1)}, u32[]{:S(2)}, u32[]{:S(2)}) collective-permute-start(bf16[512,2,128]{0,2,1:T(8,128)(2,1)S(1)} %fusion.91), channel_id=1, source_target_pairs={{0,16},{1,17},{2,18},{3,19},{4,20},{5,21},{6,22},{7,23},{8,24},{9,... | collective-permute-start | bytes 786440 | tf_op jit(solution)/shard_map/ppermute | solution.py:17
  91.1 1.9 collective-permute-start.2
  93.1 21.4 %collective-permute-done.12 = bf16[512,2,128]{0,2,1:T(8,128)(2,1)S(1)} collective-permute-done((bf16[512,2,128]{0,2,1:T(8,128)(2,1)S(1)}, bf16[512,2,128]{0,2,1:T(8,128)(2,1)S(1)}, u32[]{:S(2)}, u32[]{:S(2)}) %collective-permute-start.12) | collective-permute-done | bytes 262176 | tf_op jit(solution)/shard_map/ppermute | solution.py:17
  115.0 1.9 collective-permute-start.13
  118.6 1.9 collective-permute-start.18
  121.4 7.0 %collective-permute-start.3 = (bf16[512,2,128]{2,0,1:T(8,128)(2,1)S(1)}, bf16[512,2,128]{2,0,1:T(8,128)(2,1)S(1)}, u32[]{:S(2)}, u32[]{:S(2)}) collective-permute-start(bf16[512,2,128]{2,0,1:T(8,128)(2,1)S(1)} %fusion.110), channel_id=1, source_target_pairs={{0,4},{1,5},{2,6},{3,7},{4,0},{5,1},{6,2},{7,3},{8,12},{9,13},{10,... | collective-permute-start | bytes 786440 | tf_op jit(solution)/shard_map/ppermute | solution.py:17
  128.4 11.2 %collective-permute-done.13 = bf16[512,2,128]{2,0,1:T(8,128)(2,1)S(1)} collective-permute-done((bf16[512,2,128]{2,0,1:T(8,128)(2,1)S(1)}, bf16[512,2,128]{2,0,1:T(8,128)(2,1)S(1)}, u32[]{:S(2)}, u32[]{:S(2)}) %collective-permute-start.13) | collective-permute-done | bytes 262176 | tf_op jit(solution)/shard_map/ppermute | solution.py:17
  140.8 1.9 collective-permute-start.14
  144.4 4.2 collective-permute-start.19
  148.6 13.2 %collective-permute-done.3 = bf16[512,2,128]{2,0,1:T(8,128)(2,1)S(1)} collective-permute-done((bf16[512,2,128]{2,0,1:T(8,128)(2,1)S(1)}, bf16[512,2,128]{2,0,1:T(8,128)(2,1)S(1)}, u32[]{:S(2)}, u32[]{:S(2)}) %collective-permute-start.3) | collective-permute-done | bytes 262176 | tf_op jit(solution)/shard_map/ppermute | solution.py:17
  162.6 1.9 collective-permute-start.4
  164.5 3.0 collective-permute-done.14
  168.6 1.9 collective-permute-start.15
  170.7 4.4 collective-permute-done.19
  176.5 1.9 collective-permute-start.20
  178.4 22.9 %collective-permute-done.4 = bf16[512,2,128]{2,0,1:T(8,128)(2,1)S(1)} collective-permute-done((bf16[512,2,128]{2,0,1:T(8,128)(2,1)S(1)}, bf16[512,2,128]{2,0,1:T(8,128)(2,1)S(1)}, u32[]{:S(2)}, u32[]{:S(2)}) %collective-permute-start.4) | collective-permute-done | bytes 262176 | tf_op jit(solution)/shard_map/ppermute | solution.py:17
  203.0 1.9 collective-permute-start.5
  206.0 5.7 %collective-permute-start.16 = (bf16[512,2,128]{2,0,1:T(8,128)(2,1)S(1)}, bf16[512,2,128]{2,0,1:T(8,128)(2,1)S(1)}, u32[]{:S(2)}, u32[]{:S(2)}) collective-permute-start(bf16[512,2,128]{2,0,1:T(8,128)(2,1)S(1)} %fusion.87), channel_id=1, source_target_pairs={{0,1},{1,0},{2,3},{3,2},{4,5},{5,4},{6,7},{7,6},{8,9},{9,8},{10,11... | collective-permute-start | bytes 786440 | tf_op jit(solution)/shard_map/ppermute | solution.py:17
  211.7 34.8 %collective-permute-done.20 = bf16[512,2,128]{2,0,1:T(8,128)(2,1)S(1)} collective-permute-done((bf16[512,2,128]{2,0,1:T(8,128)(2,1)S(1)}, bf16[512,2,128]{2,0,1:T(8,128)(2,1)S(1)}, u32[]{:S(2)}, u32[]{:S(2)}) %collective-permute-start.20) | collective-permute-done | bytes 262176 | tf_op jit(solution)/shard_map/ppermute | solution.py:17
  247.2 2.1 fusion.150
  249.3 2.0 collective-permute-start.21
  255.8 11.4 %collective-permute-done.21 = bf16[512,2,128]{2,0,1:T(8,128)(2,1)S(1)} collective-permute-done((bf16[512,2,128]{2,0,1:T(8,128)(2,1)S(1)}, bf16[512,2,128]{2,0,1:T(8,128)(2,1)S(1)}, u32[]{:S(2)}, u32[]{:S(2)}) %collective-permute-start.21) | collective-permute-done | bytes 262176 | tf_op jit(solution)/shard_map/ppermute | solution.py:17
  270.5 47.5 %all-reduce = (f32[512]{0:T(512)}, f32[512]{0:T(512)}) all-reduce(f32[512]{0:T(512)} %multiply_reduce_fusion.3, f32[512]{0:T(512)} %get-tuple-element.49), channel_id=1, replica_groups=mesh['section'=16,'tp'=32] {'tp'}, use_global_device_ids=true, to_apply=%region_1.0 | all-reduce | flops 1024 | bytes 8192 | tf_op jit(solution)/shard_map/psum | solution.py:60
  323.7 2.1 fusion.107
  325.8 2.0 fusion.152
  327.8 2.7 collective-permute-start.6
  336.7 2.1 collective-permute-start.27
  339.1 6.9 %collective-permute-start.22 = (bf16[512,2,128]{2,0,1:T(8,128)(2,1)S(1)}, bf16[512,2,128]{2,0,1:T(8,128)(2,1)S(1)}, u32[]{:S(2)}, u32[]{:S(2)}) collective-permute-start(bf16[512,2,128]{2,0,1:T(8,128)(2,1)S(1)} %copy-done.89), channel_id=1, source_target_pairs={{0,16},{1,17},{2,18},{3,19},{4,20},{5,21},{6,22},{7,23},{8,24},{9,... | collective-permute-start | bytes 786440 | tf_op jit(solution)/shard_map/ppermute | solution.py:17
  349.2 21.5 %collective-permute-done.22 = bf16[512,2,128]{2,0,1:T(8,128)(2,1)S(1)} collective-permute-done((bf16[512,2,128]{2,0,1:T(8,128)(2,1)S(1)}, bf16[512,2,128]{2,0,1:T(8,128)(2,1)S(1)}, u32[]{:S(2)}, u32[]{:S(2)}) %collective-permute-start.22) | collective-permute-done | bytes 262176 | tf_op jit(solution)/shard_map/ppermute | solution.py:17
  376.6 3.4 collective-permute-start.28
  380.0 1.9 collective-permute-start.23
  383.4 23.9 %collective-permute-done.23 = bf16[512,2,128]{2,0,1:T(8,128)(2,1)S(1)} collective-permute-done((bf16[512,2,128]{2,0,1:T(8,128)(2,1)S(1)}, bf16[512,2,128]{2,0,1:T(8,128)(2,1)S(1)}, u32[]{:S(2)}, u32[]{:S(2)}) %collective-permute-start.23) | collective-permute-done | bytes 262176 | tf_op jit(solution)/shard_map/ppermute | solution.py:17
  412.3 4.3 collective-permute-start.29
  416.6 1.9 collective-permute-start.24
  420.0 25.7 %collective-permute-done.24 = bf16[512,2,128]{2,0,1:T(8,128)(2,1)S(1)} collective-permute-done((bf16[512,2,128]{2,0,1:T(8,128)(2,1)S(1)}, bf16[512,2,128]{2,0,1:T(8,128)(2,1)S(1)}, u32[]{:S(2)}, u32[]{:S(2)}) %collective-permute-start.24) | collective-permute-done | bytes 262176 | tf_op jit(solution)/shard_map/ppermute | solution.py:17
  448.1 3.4 collective-permute-start.9
  452.2 5.8 %collective-permute-start.30 = (bf16[512,2,128]{2,0,1:T(8,128)(2,1)S(1)}, bf16[512,2,128]{2,0,1:T(8,128)(2,1)S(1)}, u32[]{:S(2)}, u32[]{:S(2)}) collective-permute-start(bf16[512,2,128]{2,0,1:T(8,128)(2,1)S(1)} %fusion.94), channel_id=1, source_target_pairs={{0,8},{1,9},{2,10},{3,11},{4,12},{5,13},{6,14},{7,15},{8,0},{9,1},... | collective-permute-start | bytes 786440 | tf_op jit(solution)/shard_map/ppermute | solution.py:17
  458.0 1.9 collective-permute-start.25
  461.4 44.1 %collective-permute-done.30 = bf16[512,2,128]{2,0,1:T(8,128)(2,1)S(1)} collective-permute-done((bf16[512,2,128]{2,0,1:T(8,128)(2,1)S(1)}, bf16[512,2,128]{2,0,1:T(8,128)(2,1)S(1)}, u32[]{:S(2)}, u32[]{:S(2)}) %collective-permute-start.30) | collective-permute-done | bytes 262176 | tf_op jit(solution)/shard_map/ppermute | solution.py:17
  505.8 6.4 %collective-permute-start.31 = (bf16[512,2,128]{2,0,1:T(8,128)(2,1)S(1)}, bf16[512,2,128]{2,0,1:T(8,128)(2,1)}, u32[]{:S(2)}, u32[]{:S(2)}) collective-permute-start(bf16[512,2,128]{2,0,1:T(8,128)(2,1)S(1)} %fusion.93), channel_id=1, source_target_pairs={{0,16},{1,17},{2,18},{3,19},{4,20},{5,21},{6,22},{7,23},{8,24},{9,... | collective-permute-start | bytes 786440 | tf_op jit(solution)/shard_map/ppermute | solution.py:17
  515.5 7.7 %collective-permute-start.10 = (bf16[512,2,128]{2,0,1:T(8,128)(2,1)S(1)}, bf16[512,2,128]{2,0,1:T(8,128)(2,1)}, u32[]{:S(2)}, u32[]{:S(2)}) collective-permute-start(bf16[512,2,128]{2,0,1:T(8,128)(2,1)S(1)} %fusion.103), channel_id=1, source_target_pairs={{0,16},{1,17},{2,18},{3,19},{4,20},{5,21},{6,22},{7,23},{8,24},{9,... | collective-permute-start | bytes 786440 | tf_op jit(solution)/shard_map/ppermute | solution.py:17
  523.2 3.0 collective-permute-start.26
  538.4 11.2 %collective-permute-done.10 = bf16[512,2,128]{2,0,1:T(8,128)(2,1)} collective-permute-done((bf16[512,2,128]{2,0,1:T(8,128)(2,1)S(1)}, bf16[512,2,128]{2,0,1:T(8,128)(2,1)}, u32[]{:S(2)}, u32[]{:S(2)}) %collective-permute-start.10) | collective-permute-done | bytes 262176 | tf_op jit(solution)/shard_map/ppermute | solution.py:17
  (407 shorter events, 91.4 us)
Async XLA Ops:
  2.5 69.6 %collective-permute-start = (bf16[1,512,256]{1,2,0:T(8,128)(2,1)}, bf16[1,512,256]{1,2,0:T(8,128)(2,1)S(1)}, u32[]{:S(2)}, u32[]{:S(2)}) collective-permute-start(bf16[1,512,256]{1,2,0:T(8,128)(2,1)} %copy.52), channel_id=1, source_target_pairs={{0,32},{32,64},{64,96},{96,128},{128,160},{160,192},{192,224},{224... | collective-permute-start | bytes 786440 | tf_op jit(solution)/shard_map/ppermute | solution.py:23
  7.4 73.2 %collective-permute-start.11 = (bf16[1,512,256]{1,2,0:T(8,128)(2,1)}, bf16[1,512,256]{1,2,0:T(8,128)(2,1)S(1)}, u32[]{:S(2)}, u32[]{:S(2)}) collective-permute-start(bf16[1,512,256]{1,2,0:T(8,128)(2,1)} %copy.57), channel_id=1, source_target_pairs={{0,480},{32,0},{64,32},{96,64},{128,96},{160,128},{192,160},{224,1... | collective-permute-start | bytes 786440 | tf_op jit(solution)/shard_map/ppermute | solution.py:23
  13.8 100.9 %copy-start.16 = (bf16[1,1,1,256,128]{4,3,2,1,0:T(8,128)(2,1)}, bf16[1,1,1,256,128]{4,3,2,1,0:T(8,128)(2,1)S(1)}, u32[]{:S(2)}) copy-start(bf16[1,1,1,256,128]{4,3,2,1,0:T(8,128)(2,1)S(1)} %get-tuple-element.47) | copy-start | bytes 196612
  13.8 103.4 %copy-start.18 = (bf16[1,1,1,256,128]{4,3,2,1,0:T(8,128)(2,1)}, bf16[1,1,1,256,128]{4,3,2,1,0:T(8,128)(2,1)S(1)}, u32[]{:S(2)}) copy-start(bf16[1,1,1,256,128]{4,3,2,1,0:T(8,128)(2,1)S(1)} %get-tuple-element.44) | copy-start | bytes 196612
  13.8 126.1 %copy-start.20 = (bf16[1,1,1,256,128]{4,3,2,1,0:T(8,128)(2,1)}, bf16[1,1,1,256,128]{4,3,2,1,0:T(8,128)(2,1)S(1)}, u32[]{:S(2)}) copy-start(bf16[1,1,1,256,128]{4,3,2,1,0:T(8,128)(2,1)S(1)} %get-tuple-element.37) | copy-start | bytes 196612
  13.8 129.1 %copy-start.22 = (bf16[1,1,1,256,128]{4,3,2,1,0:T(8,128)(2,1)}, bf16[1,1,1,256,128]{4,3,2,1,0:T(8,128)(2,1)S(1)}, u32[]{:S(2)}) copy-start(bf16[1,1,1,256,128]{4,3,2,1,0:T(8,128)(2,1)S(1)} %get-tuple-element.43) | copy-start | bytes 196612
  13.8 153.8 %copy-start.24 = (bf16[1,1,1,256,128]{4,3,2,1,0:T(8,128)(2,1)}, bf16[1,1,1,256,128]{4,3,2,1,0:T(8,128)(2,1)S(1)}, u32[]{:S(2)}) copy-start(bf16[1,1,1,256,128]{4,3,2,1,0:T(8,128)(2,1)S(1)} %get-tuple-element.38) | copy-start | bytes 196612
  13.9 161.3 %copy-start.26 = (bf16[1,1,1,256,128]{4,3,2,1,0:T(8,128)(2,1)}, bf16[1,1,1,256,128]{4,3,2,1,0:T(8,128)(2,1)S(1)}, u32[]{:S(2)}) copy-start(bf16[1,1,1,256,128]{4,3,2,1,0:T(8,128)(2,1)S(1)} %get-tuple-element.42) | copy-start | bytes 196612
  13.9 191.3 %copy-start.28 = (bf16[1,1,1,256,128]{4,3,2,1,0:T(8,128)(2,1)}, bf16[1,1,1,256,128]{4,3,2,1,0:T(8,128)(2,1)S(1)}, u32[]{:S(2)}) copy-start(bf16[1,1,1,256,128]{4,3,2,1,0:T(8,128)(2,1)S(1)} %get-tuple-element.39) | copy-start | bytes 196612
  13.9 232.6 %copy-start.30 = (bf16[1,1,1,256,128]{4,3,2,1,0:T(8,128)(2,1)}, bf16[1,1,1,256,128]{4,3,2,1,0:T(8,128)(2,1)S(1)}, u32[]{:S(2)}) copy-start(bf16[1,1,1,256,128]{4,3,2,1,0:T(8,128)(2,1)S(1)} %get-tuple-element.41) | copy-start | bytes 196612
  73.7 15.6 %collective-permute-start.1 = (bf16[512,2,128]{2,0,1:T(8,128)(2,1)S(1)}, bf16[512,2,128]{2,0,1:T(8,128)(2,1)}, u32[]{:S(2)}, u32[]{:S(2)}) collective-permute-start(bf16[512,2,128]{2,0,1:T(8,128)(2,1)S(1)} %fusion.92), channel_id=1, source_target_pairs={{0,1},{1,0},{2,3},{3,2},{4,5},{5,4},{6,7},{7,6},{8,9},{9,8},{10,11... | collective-permute-start | bytes 786440 | tf_op jit(solution)/shard_map/ppermute | solution.py:17
  78.5 38.7 %collective-permute-start.17 = (bf16[512,2,128]{2,0,1:T(8,128)(2,1)S(1)}, bf16[512,2,128]{2,0,1:T(8,128)(2,1)S(1)}, u32[]{:S(2)}, u32[]{:S(2)}) collective-permute-start(bf16[512,2,128]{2,0,1:T(8,128)(2,1)S(1)} %fusion.102), channel_id=1, source_target_pairs={{0,1},{1,0},{2,3},{3,2},{4,5},{5,4},{6,7},{7,6},{8,9},{9,8},{10,11... | collective-permute-start | bytes 786440 | tf_op jit(solution)/shard_map/ppermute | solution.py:17
  81.5 33.0 %collective-permute-start.12 = (bf16[512,2,128]{0,2,1:T(8,128)(2,1)S(1)}, bf16[512,2,128]{0,2,1:T(8,128)(2,1)S(1)}, u32[]{:S(2)}, u32[]{:S(2)}) collective-permute-start(bf16[512,2,128]{0,2,1:T(8,128)(2,1)S(1)} %fusion.91), channel_id=1, source_target_pairs={{0,16},{1,17},{2,18},{3,19},{4,20},{5,21},{6,22},{7,23},{8,24},{9,... | collective-permute-start | bytes 786440 | tf_op jit(solution)/shard_map/ppermute | solution.py:17
  89.9 24.6 %copy-start.66 = (bf16[1,1,1,256,128]{4,3,2,1,0:T(8,128)(2,1)S(1)}, bf16[1,1,1,256,128]{4,3,2,1,0:T(8,128)(2,1)}, u32[]{:S(2)}) copy-start(bf16[1,1,1,256,128]{4,3,2,1,0:T(8,128)(2,1)} %get-tuple-element.34) | copy-start | bytes 196612
  91.1 29.4 %collective-permute-start.2 = (bf16[512,2,128]{2,0,1:T(8,128)(2,1)S(1)}, bf16[512,2,128]{2,0,1:T(8,128)(2,1)S(1)}, u32[]{:S(2)}, u32[]{:S(2)}) collective-permute-start(bf16[512,2,128]{2,0,1:T(8,128)(2,1)S(1)} %fusion.111), channel_id=1, source_target_pairs={{0,2},{1,3},{2,0},{3,1},{4,6},{5,7},{6,4},{7,5},{8,10},{9,11},{10,... | collective-permute-start | bytes 786440 | tf_op jit(solution)/shard_map/ppermute | solution.py:17
  115.0 24.6 %collective-permute-start.13 = (bf16[512,2,128]{2,0,1:T(8,128)(2,1)S(1)}, bf16[512,2,128]{2,0,1:T(8,128)(2,1)S(1)}, u32[]{:S(2)}, u32[]{:S(2)}) collective-permute-start(bf16[512,2,128]{2,0,1:T(8,128)(2,1)S(1)} %fusion.90), channel_id=1, source_target_pairs={{0,8},{1,9},{2,10},{3,11},{4,12},{5,13},{6,14},{7,15},{8,0},{9,1},... | collective-permute-start | bytes 786440 | tf_op jit(solution)/shard_map/ppermute | solution.py:17
  118.6 24.3 %collective-permute-start.18 = (bf16[512,2,128]{2,0,1:T(8,128)(2,1)S(1)}, bf16[512,2,128]{2,0,1:T(8,128)(2,1)S(1)}, u32[]{:S(2)}, u32[]{:S(2)}) collective-permute-start(bf16[512,2,128]{2,0,1:T(8,128)(2,1)S(1)} %fusion.101), channel_id=1, source_target_pairs={{0,2},{1,3},{2,0},{3,1},{4,6},{5,7},{6,4},{7,5},{8,10},{9,11},{10,... | collective-permute-start | bytes 786440 | tf_op jit(solution)/shard_map/ppermute | solution.py:17
  121.4 40.4 %collective-permute-start.3 = (bf16[512,2,128]{2,0,1:T(8,128)(2,1)S(1)}, bf16[512,2,128]{2,0,1:T(8,128)(2,1)S(1)}, u32[]{:S(2)}, u32[]{:S(2)}) collective-permute-start(bf16[512,2,128]{2,0,1:T(8,128)(2,1)S(1)} %fusion.110), channel_id=1, source_target_pairs={{0,4},{1,5},{2,6},{3,7},{4,0},{5,1},{6,2},{7,3},{8,12},{9,13},{10,... | collective-permute-start | bytes 786440 | tf_op jit(solution)/shard_map/ppermute | solution.py:17
  140.8 26.7 %collective-permute-start.14 = (bf16[512,2,128]{2,0,1:T(8,128)(2,1)S(1)}, bf16[512,2,128]{2,0,1:T(8,128)(2,1)S(1)}, u32[]{:S(2)}, u32[]{:S(2)}) collective-permute-start(bf16[512,2,128]{2,0,1:T(8,128)(2,1)S(1)} %fusion.89), channel_id=1, source_target_pairs={{0,4},{1,5},{2,6},{3,7},{4,0},{5,1},{6,2},{7,3},{8,12},{9,13},{10,... | collective-permute-start | bytes 786440 | tf_op jit(solution)/shard_map/ppermute | solution.py:17
  144.4 30.8 %collective-permute-start.19 = (bf16[512,2,128]{2,0,1:T(8,128)(2,1)S(1)}, bf16[512,2,128]{2,0,1:T(8,128)(2,1)S(1)}, u32[]{:S(2)}, u32[]{:S(2)}) collective-permute-start(bf16[512,2,128]{2,0,1:T(8,128)(2,1)S(1)} %fusion.100), channel_id=1, source_target_pairs={{0,4},{1,5},{2,6},{3,7},{4,0},{5,1},{6,2},{7,3},{8,12},{9,13},{10,... | collective-permute-start | bytes 786440 | tf_op jit(solution)/shard_map/ppermute | solution.py:17
  162.6 38.8 %collective-permute-start.4 = (bf16[512,2,128]{2,0,1:T(8,128)(2,1)S(1)}, bf16[512,2,128]{2,0,1:T(8,128)(2,1)S(1)}, u32[]{:S(2)}, u32[]{:S(2)}) collective-permute-start(bf16[512,2,128]{2,0,1:T(8,128)(2,1)S(1)} %fusion.109), channel_id=1, source_target_pairs={{0,8},{1,9},{2,10},{3,11},{4,12},{5,13},{6,14},{7,15},{8,0},{9,1},... | collective-permute-start | bytes 786440 | tf_op jit(solution)/shard_map/ppermute | solution.py:17
  168.6 36.3 %collective-permute-start.15 = (bf16[512,2,128]{2,0,1:T(8,128)(2,1)S(1)}, bf16[512,2,128]{2,0,1:T(8,128)(2,1)S(1)}, u32[]{:S(2)}, u32[]{:S(2)}) collective-permute-start(bf16[512,2,128]{2,0,1:T(8,128)(2,1)S(1)} %fusion.88), channel_id=1, source_target_pairs={{0,2},{1,3},{2,0},{3,1},{4,6},{5,7},{6,4},{7,5},{8,10},{9,11},{10,... | collective-permute-start | bytes 786440 | tf_op jit(solution)/shard_map/ppermute | solution.py:17
  176.5 70.0 %collective-permute-start.20 = (bf16[512,2,128]{2,0,1:T(8,128)(2,1)S(1)}, bf16[512,2,128]{2,0,1:T(8,128)(2,1)S(1)}, u32[]{:S(2)}, u32[]{:S(2)}) collective-permute-start(bf16[512,2,128]{2,0,1:T(8,128)(2,1)S(1)} %fusion.99), channel_id=1, source_target_pairs={{0,8},{1,9},{2,10},{3,11},{4,12},{5,13},{6,14},{7,15},{8,0},{9,1},... | collective-permute-start | bytes 786440 | tf_op jit(solution)/shard_map/ppermute | solution.py:17
  203.0 115.7 %collective-permute-start.5 = (bf16[512,2,128]{2,0,1:T(8,128)(2,1)}, bf16[512,2,128]{2,0,1:T(8,128)(2,1)}, u32[]{:S(2)}, u32[]{:S(2)}) collective-permute-start(bf16[512,2,128]{2,0,1:T(8,128)(2,1)} %fusion.108), channel_id=1, source_target_pairs={{0,16},{1,17},{2,18},{3,19},{4,20},{5,21},{6,22},{7,23},{8,24},{9,... | collective-permute-start | bytes 786440 | tf_op jit(solution)/shard_map/ppermute | solution.py:17
  206.0 41.2 %copy-start.56 = (bf16[1,1,1,256,128]{4,3,2,1,0:T(8,128)(2,1)S(1)}, bf16[1,1,1,256,128]{4,3,2,1,0:T(8,128)(2,1)}, u32[]{:S(2)}) copy-start(bf16[1,1,1,256,128]{4,3,2,1,0:T(8,128)(2,1)} %get-tuple-element.28) | copy-start | bytes 196612
  206.0 46.3 %collective-permute-start.16 = (bf16[512,2,128]{2,0,1:T(8,128)(2,1)S(1)}, bf16[512,2,128]{2,0,1:T(8,128)(2,1)S(1)}, u32[]{:S(2)}, u32[]{:S(2)}) collective-permute-start(bf16[512,2,128]{2,0,1:T(8,128)(2,1)S(1)} %fusion.87), channel_id=1, source_target_pairs={{0,1},{1,0},{2,3},{3,2},{4,5},{5,4},{6,7},{7,6},{8,9},{9,8},{10,11... | collective-permute-start | bytes 786440 | tf_op jit(solution)/shard_map/ppermute | solution.py:17
  249.3 17.9 %collective-permute-start.21 = (bf16[512,2,128]{2,0,1:T(8,128)(2,1)S(1)}, bf16[512,2,128]{2,0,1:T(8,128)(2,1)S(1)}, u32[]{:S(2)}, u32[]{:S(2)}) collective-permute-start(bf16[512,2,128]{2,0,1:T(8,128)(2,1)S(1)} %fusion.98), channel_id=1, source_target_pairs={{0,16},{1,17},{2,18},{3,19},{4,20},{5,21},{6,22},{7,23},{8,24},{9,... | collective-permute-start | bytes 786440 | tf_op jit(solution)/shard_map/ppermute | solution.py:17
  327.8 43.5 %collective-permute-start.6 = (bf16[512,2,128]{2,0,1:T(8,128)(2,1)}, bf16[512,2,128]{2,0,1:T(8,128)(2,1)}, u32[]{:S(2)}, u32[]{:S(2)}) collective-permute-start(bf16[512,2,128]{2,0,1:T(8,128)(2,1)} %fusion.107), channel_id=1, source_target_pairs={{0,1},{1,0},{2,3},{3,2},{4,5},{5,4},{6,7},{7,6},{8,9},{9,8},{10,11... | collective-permute-start | bytes 786440 | tf_op jit(solution)/shard_map/ppermute | solution.py:17
  336.7 39.4 %collective-permute-start.27 = (bf16[512,2,128]{2,0,1:T(8,128)(2,1)S(1)}, bf16[512,2,128]{2,0,1:T(8,128)(2,1)S(1)}, u32[]{:S(2)}, u32[]{:S(2)}) collective-permute-start(bf16[512,2,128]{2,0,1:T(8,128)(2,1)S(1)} %fusion.97), channel_id=1, source_target_pairs={{0,1},{1,0},{2,3},{3,2},{4,5},{5,4},{6,7},{7,6},{8,9},{9,8},{10,11... | collective-permute-start | bytes 786440 | tf_op jit(solution)/shard_map/ppermute | solution.py:17
  339.1 31.7 %collective-permute-start.22 = (bf16[512,2,128]{2,0,1:T(8,128)(2,1)S(1)}, bf16[512,2,128]{2,0,1:T(8,128)(2,1)S(1)}, u32[]{:S(2)}, u32[]{:S(2)}) collective-permute-start(bf16[512,2,128]{2,0,1:T(8,128)(2,1)S(1)} %copy-done.89), channel_id=1, source_target_pairs={{0,16},{1,17},{2,18},{3,19},{4,20},{5,21},{6,22},{7,23},{8,24},{9,... | collective-permute-start | bytes 786440 | tf_op jit(solution)/shard_map/ppermute | solution.py:17
  373.9 33.9 %collective-permute-start.7 = (bf16[512,2,128]{2,0,1:T(8,128)(2,1)S(1)}, bf16[512,2,128]{2,0,1:T(8,128)(2,1)S(1)}, u32[]{:S(2)}, u32[]{:S(2)}) collective-permute-start(bf16[512,2,128]{2,0,1:T(8,128)(2,1)S(1)} %fusion.106), channel_id=1, source_target_pairs={{0,2},{1,3},{2,0},{3,1},{4,6},{5,7},{6,4},{7,5},{8,10},{9,11},{10,... | collective-permute-start | bytes 786440 | tf_op jit(solution)/shard_map/ppermute | solution.py:17
  376.6 35.2 %collective-permute-start.28 = (bf16[512,2,128]{2,0,1:T(8,128)(2,1)S(1)}, bf16[512,2,128]{2,0,1:T(8,128)(2,1)S(1)}, u32[]{:S(2)}, u32[]{:S(2)}) collective-permute-start(bf16[512,2,128]{2,0,1:T(8,128)(2,1)S(1)} %fusion.96), channel_id=1, source_target_pairs={{0,2},{1,3},{2,0},{3,1},{4,6},{5,7},{6,4},{7,5},{8,10},{9,11},{10,... | collective-permute-start | bytes 786440 | tf_op jit(solution)/shard_map/ppermute | solution.py:17
  380.0 27.3 %collective-permute-start.23 = (bf16[512,2,128]{2,0,1:T(8,128)(2,1)S(1)}, bf16[512,2,128]{2,0,1:T(8,128)(2,1)S(1)}, u32[]{:S(2)}, u32[]{:S(2)}) collective-permute-start(bf16[512,2,128]{2,0,1:T(8,128)(2,1)S(1)} %fusion.84), channel_id=1, source_target_pairs={{0,8},{1,9},{2,10},{3,11},{4,12},{5,13},{6,14},{7,15},{8,0},{9,1},... | collective-permute-start | bytes 786440 | tf_op jit(solution)/shard_map/ppermute | solution.py:17
  383.3 24.1 %copy-start.27 = (bf16[1,1,1,256,128]{4,3,2,1,0:T(8,128)(2,1)S(1)}, bf16[1,1,1,256,128]{4,3,2,1,0:T(8,128)(2,1)}, u32[]{:S(2)}) copy-start(bf16[1,1,1,256,128]{4,3,2,1,0:T(8,128)(2,1)} %copy-done.26) | copy-start | bytes 196612
  383.4 24.1 %copy-start.105 = (f32[2]{0:T(128)S(1)}, f32[2]{0:T(128)}, u32[]{:S(2)}) copy-start(f32[2]{0:T(128)} %get-tuple-element.18) | copy-start | bytes 28
  409.6 36.6 %collective-permute-start.8 = (bf16[512,2,128]{2,0,1:T(8,128)(2,1)S(1)}, bf16[512,2,128]{2,0,1:T(8,128)(2,1)S(1)}, u32[]{:S(2)}, u32[]{:S(2)}) collective-permute-start(bf16[512,2,128]{2,0,1:T(8,128)(2,1)S(1)} %fusion.105), channel_id=1, source_target_pairs={{0,4},{1,5},{2,6},{3,7},{4,0},{5,1},{6,2},{7,3},{8,12},{9,13},{10,... | collective-permute-start | bytes 786440 | tf_op jit(solution)/shard_map/ppermute | solution.py:17
  412.3 39.4 %collective-permute-start.29 = (bf16[512,2,128]{2,0,1:T(8,128)(2,1)S(1)}, bf16[512,2,128]{2,0,1:T(8,128)(2,1)S(1)}, u32[]{:S(2)}, u32[]{:S(2)}) collective-permute-start(bf16[512,2,128]{2,0,1:T(8,128)(2,1)S(1)} %fusion.95), channel_id=1, source_target_pairs={{0,4},{1,5},{2,6},{3,7},{4,0},{5,1},{6,2},{7,3},{8,12},{9,13},{10,... | collective-permute-start | bytes 786440 | tf_op jit(solution)/shard_map/ppermute | solution.py:17
  416.6 29.1 %collective-permute-start.24 = (bf16[512,2,128]{2,0,1:T(8,128)(2,1)S(1)}, bf16[512,2,128]{2,0,1:T(8,128)(2,1)S(1)}, u32[]{:S(2)}, u32[]{:S(2)}) collective-permute-start(bf16[512,2,128]{2,0,1:T(8,128)(2,1)S(1)} %fusion.83), channel_id=1, source_target_pairs={{0,4},{1,5},{2,6},{3,7},{4,0},{5,1},{6,2},{7,3},{8,12},{9,13},{10,... | collective-permute-start | bytes 786440 | tf_op jit(solution)/shard_map/ppermute | solution.py:17
  419.7 25.9 %copy-start.49 = (bf16[1,1,1,256,128]{4,3,2,1,0:T(8,128)(2,1)S(1)}, bf16[1,1,1,256,128]{4,3,2,1,0:T(8,128)(2,1)}, u32[]{:S(2)}) copy-start(bf16[1,1,1,256,128]{4,3,2,1,0:T(8,128)(2,1)} %get-tuple-element.30) | copy-start | bytes 196612
  420.0 26.0 %copy-start.23 = (bf16[1,1,1,256,128]{4,3,2,1,0:T(8,128)(2,1)S(1)}, bf16[1,1,1,256,128]{4,3,2,1,0:T(8,128)(2,1)}, u32[]{:S(2)}) copy-start(bf16[1,1,1,256,128]{4,3,2,1,0:T(8,128)(2,1)} %copy-done.22) | copy-start | bytes 196612
  420.0 26.0 %copy-start.101 = (f32[2]{0:T(128)S(1)}, f32[2]{0:T(128)}, u32[]{:S(2)}) copy-start(f32[2]{0:T(128)} %get-tuple-element.19) | copy-start | bytes 28
  448.1 67.1 %collective-permute-start.9 = (bf16[512,2,128]{2,0,1:T(8,128)(2,1)S(1)}, bf16[512,2,128]{2,0,1:T(8,128)(2,1)S(1)}, u32[]{:S(2)}, u32[]{:S(2)}) collective-permute-start(bf16[512,2,128]{2,0,1:T(8,128)(2,1)S(1)} %fusion.104), channel_id=1, source_target_pairs={{0,8},{1,9},{2,10},{3,11},{4,12},{5,13},{6,14},{7,15},{8,0},{9,1},... | collective-permute-start | bytes 786440 | tf_op jit(solution)/shard_map/ppermute | solution.py:17
  452.2 53.3 %collective-permute-start.30 = (bf16[512,2,128]{2,0,1:T(8,128)(2,1)S(1)}, bf16[512,2,128]{2,0,1:T(8,128)(2,1)S(1)}, u32[]{:S(2)}, u32[]{:S(2)}) collective-permute-start(bf16[512,2,128]{2,0,1:T(8,128)(2,1)S(1)} %fusion.94), channel_id=1, source_target_pairs={{0,8},{1,9},{2,10},{3,11},{4,12},{5,13},{6,14},{7,15},{8,0},{9,1},... | collective-permute-start | bytes 786440 | tf_op jit(solution)/shard_map/ppermute | solution.py:17
  458.0 55.1 %collective-permute-start.25 = (bf16[512,2,128]{2,0,1:T(8,128)(2,1)S(1)}, bf16[512,2,128]{2,0,1:T(8,128)(2,1)S(1)}, u32[]{:S(2)}, u32[]{:S(2)}) collective-permute-start(bf16[512,2,128]{2,0,1:T(8,128)(2,1)S(1)} %fusion.82), channel_id=1, source_target_pairs={{0,2},{1,3},{2,0},{3,1},{4,6},{5,7},{6,4},{7,5},{8,10},{9,11},{10,... | collective-permute-start | bytes 786440 | tf_op jit(solution)/shard_map/ppermute | solution.py:17
  461.2 44.3 %copy-start.17 = (bf16[1,1,1,256,128]{4,3,2,1,0:T(8,128)(2,1)S(1)}, bf16[1,1,1,256,128]{4,3,2,1,0:T(8,128)(2,1)}, u32[]{:S(2)}) copy-start(bf16[1,1,1,256,128]{4,3,2,1,0:T(8,128)(2,1)} %copy-done.16) | copy-start | bytes 196612
  505.8 49.7 %collective-permute-start.31 = (bf16[512,2,128]{2,0,1:T(8,128)(2,1)S(1)}, bf16[512,2,128]{2,0,1:T(8,128)(2,1)}, u32[]{:S(2)}, u32[]{:S(2)}) collective-permute-start(bf16[512,2,128]{2,0,1:T(8,128)(2,1)S(1)} %fusion.93), channel_id=1, source_target_pairs={{0,16},{1,17},{2,18},{3,19},{4,20},{5,21},{6,22},{7,23},{8,24},{9,... | collective-permute-start | bytes 786440 | tf_op jit(solution)/shard_map/ppermute | solution.py:17
  515.5 34.2 %collective-permute-start.10 = (bf16[512,2,128]{2,0,1:T(8,128)(2,1)S(1)}, bf16[512,2,128]{2,0,1:T(8,128)(2,1)}, u32[]{:S(2)}, u32[]{:S(2)}) collective-permute-start(bf16[512,2,128]{2,0,1:T(8,128)(2,1)S(1)} %fusion.103), channel_id=1, source_target_pairs={{0,16},{1,17},{2,18},{3,19},{4,20},{5,21},{6,22},{7,23},{8,24},{9,... | collective-permute-start | bytes 786440 | tf_op jit(solution)/shard_map/ppermute | solution.py:17
  523.2 5.8 %collective-permute-start.26 = (bf16[512,2,128]{2,0,1:T(8,128)(2,1)S(1)}, bf16[512,2,128]{2,0,1:T(8,128)(2,1)S(1)}, u32[]{:S(2)}, u32[]{:S(2)}) collective-permute-start(bf16[512,2,128]{2,0,1:T(8,128)(2,1)S(1)} %fusion.81), channel_id=1, source_target_pairs={{0,1},{1,0},{2,3},{3,2},{4,5},{5,4},{6,7},{7,6},{8,9},{9,8},{10,11... | collective-permute-start | bytes 786440 | tf_op jit(solution)/shard_map/ppermute | solution.py:17
  (106 other events, 374.6 us)

commit v2 on v1

v2 whole, which is shorter than its diff:
```python
import functools

import jax
import jax.numpy as jnp
from jax import lax
from jax.experimental import pallas as pl
from jax.experimental.pallas import tpu as pltpu
from jax.sharding import PartitionSpec as P

EPSILON = 1e-05
GELU_C = 0.7978845608028654
GELU_A = 0.044715
BLOCK = 128
ROWS = 256
MESH = pl.DeviceIdType.MESH
F32 = jnp.float32
BF16 = jnp.bfloat16


def gelu_value(v):
    inner = GELU_C * (v + GELU_A * v * v * v)
    return 0.5 * v * (1.0 + jnp.tanh(inner))


def gelu_slope(v):
    inner = GELU_C * (v + GELU_A * v * v * v)
    tanh_val = jnp.tanh(inner)
    return 0.5 * (1.0 + tanh_val) + 0.5 * v * (1.0 - tanh_val * tanh_val) * GELU_C * (
        1.0 + 3.0 * GELU_A * v * v
    )


def contract(a, b, da, db):
    return lax.dot_general(a, b, (((da,), (db,)), ((), ())), preferred_element_type=F32)


def columns(l):
    return slice(l * BLOCK, (l + 1) * BLOCK)


def kernel(
    sections,
    bits,
    order,
    sent,
    stash,
    gback,
    gain,
    selfw,
    partw,
    out_act,
    grad_in,
    gself,
    gpart,
    ggain,
    arr,
    ret,
    s_v,
    s_o,
    a_v,
    a_o,
    b_g,
    b_t,
    b_o,
    own,
    pre,
    acc,
    rs_col,
    rs_row,
    st_v,
    st_o,
    send_sem,
    recv_sem,
):
    tokens, width = stash.shape
    factors = bits + 1
    last = factors - 1
    rows_step = min(ROWS, tokens)
    total_width = float((2**bits) * width)
    sec = lax.axis_index("section")
    tp = lax.axis_index("tp")
    ahead = lax.rem(sec + 1, sections)
    behind = lax.rem(sec + sections - 1, sections)
    peers = []
    for j in range(bits):
        m = 2**j
        peers.append(tp + m - 2 * m * ((tp // m) % 2))

    barrier = pltpu.get_barrier_semaphore()
    for peer in peers:
        pl.semaphore_signal(barrier, inc=1, device_id=(sec, peer), device_id_type=MESH)
    for other in (ahead, behind):
        pl.semaphore_signal(barrier, inc=1, device_id=(other, tp), device_id_type=MESH)
    pl.semaphore_wait(barrier, bits + 2)

    pending = []

    def send(src, dst, where):
        n = len(pending)
        copy = pltpu.make_async_remote_copy(
            src_ref=src,
            dst_ref=dst,
            send_sem=send_sem.at[n],
            recv_sem=recv_sem.at[n],
            device_id=where,
            device_id_type=MESH,
        )
        copy.start()
        pending.append(copy)
        return copy

    def over_rows(body):
        def one(i, carry):
            body(pl.ds(pl.multiple_of(i * rows_step, rows_step), rows_step))
            return carry

        lax.fori_loop(0, tokens // rows_step, one, 0)

    def local_weights(p):
        f = p * factors
        top = jnp.concatenate([selfw[f, columns(0), :], partw[f, columns(1), :]], axis=1)
        low = jnp.concatenate([partw[f, columns(0), :], selfw[f, columns(1), :]], axis=1)
        return jnp.concatenate([top, low], axis=0)

    def stacked(p, k, l):
        f = p * factors + k
        return jnp.concatenate([selfw[f, columns(l), :], partw[f, columns(l), :]], axis=0)

    def forward(p, k, v, o, emit):
        def body(rows):
            if k == 0:
                both = contract(v[rows, :], local_weights(p), 1, 0)
                for l in range(2):
                    emit(rows, l, both[:, columns(l)])
                return
            for l in range(2):
                lhs = jnp.concatenate([v[rows, columns(l)], o[rows, columns(l)]], axis=1)
                emit(rows, l, contract(lhs, stacked(p, k, l), 1, 0))

        over_rows(body)

    def row_sums(values):
        return jnp.sum(values.T, axis=0, keepdims=True)

    def as_column(row):
        return jnp.broadcast_to(row, (BLOCK, tokens)).T

    class Total:
        def __init__(self, slot):
            self.slot, self.at = slot, 0

        def begin(self, values):
            st_v[self.slot, 0] = row_sums(values)

        def send(self, peer):
            n = self.at
            self.copy = send(st_v.at[self.slot, n], st_o.at[self.slot, n], (sec, peer))

        def absorb(self):
            n = self.at
            self.copy.wait_recv()
            st_v[self.slot, n + 1] = st_v[self.slot, n] + st_o[self.slot, n]
            self.at = n + 1

        def value(self):
            return st_v[self.slot, self.at]

    def scale_of(total):
        return lax.rsqrt(total.value() / total_width + EPSILON)

    def start_norm(x, v, total):
        def body(rows):
            squares = None
            for l in range(2):
                part = x[rows, columns(l)].astype(F32)
                v[rows, columns(l)] = (part * gain[:, columns(l)]).astype(BF16)
                squares = part * part if squares is None else squares + part * part
            acc[rows, :] = squares

        over_rows(body)
        total.begin(acc[...])

    def forward_chain(x, wait_x, v, o, slot, finish_first, finish_second, keep):
        def store(p, k):
            def emit(rows, l, value):
                v[p, k, rows, columns(l)] = value.astype(BF16)

            return emit

        total = Total(slot)
        if wait_x is not None:
            wait_x.wait_recv()
        start_norm(x, v.at[0, 0], total)
        for p in range(2):
            forward(p, 0, v.at[p, 0], None, store(p, 1))
            for k in range(1, factors):
                copy = send(v.at[p, k], o.at[p, k - 1], (sec, peers[k - 1]))
                if p == 0:
                    total.send(peers[k - 1])
                yield
                copy.wait_recv()
                if p == 0:
                    total.absorb()
                if k < last:
                    forward(p, k, v.at[p, k], o.at[p, k - 1], store(p, k + 1))
                elif p == 0:
                    forward(p, k, v.at[p, k], o.at[p, k - 1], finish_first(total))
                elif keep:
                    forward(p, k, v.at[p, k], o.at[p, k - 1], finish_second)
        yield

    def stash_first(total):
        scale = scale_of(total)
        rs_row[...] = scale
        rs_col[...] = as_column(scale)

        def emit(rows, l, value):
            value = value * rs_col[rows, :]
            pre[rows, columns(l)] = value
            s_v[1, 0, rows, columns(l)] = gelu_value(value).astype(BF16)

        return emit

    def arriving_first(total):
        acc[...] = as_column(scale_of(total))

        def emit(rows, l, value):
            a_v[1, 0, rows, columns(l)] = gelu_value(value * acc[rows, :]).astype(BF16)

        return emit

    def arriving_second(rows, l, value):
        out_act[rows, columns(l)] = (arr[rows, columns(l)].astype(F32) + value).astype(BF16)

    def backward_chain():
        from_ahead.wait_recv()
        total = Total(2)
        for p in (1, 0):
            for k in range(last, 0, -1):
                g = ret if (p == 1 and k == last) else b_g.at[p, k]
                term = b_t.at[p, k - 1]

                def split(rows, g=g, term=term, p=p, k=k):
                    for l in range(2):
                        both = contract(g[rows, columns(l)], stacked(p, k, l), 1, 1)
                        own[rows, columns(l)] = both[:, columns(0)]
                        term[rows, columns(l)] = both[:, columns(1)].astype(BF16)

                over_rows(split)
                copy = send(term, b_o.at[p, k - 1], (sec, peers[k - 1]))
                if p == 0:
                    total.send(peers[k - 1])
                yield
                copy.wait_recv()
                if p == 0:
                    total.absorb()

                def join(rows, p=p, k=k):
                    b_g[p, k - 1, rows, :] = (
                        own[rows, :] + b_o[p, k - 1, rows, :].astype(F32)
                    ).astype(BF16)

                over_rows(join)

            if p == 1:

                def middle(rows):
                    dh = contract(b_g[1, 0, rows, :], local_weights(1), 1, 1)
                    products = None
                    for l in range(2):
                        a = pre[rows, columns(l)]
                        da = dh[:, columns(l)] * gelu_slope(a)
                        products = da * a if products is None else products + da * a
                        b_g[0, last, rows, columns(l)] = (da * rs_col[rows, :]).astype(BF16)
                    acc[rows, :] = products

                over_rows(middle)
                total.begin(acc[...])
        scale = rs_row[...]
        acc[...] = as_column(scale * scale * total.value() / total_width)
        ggain[...] = jnp.zeros_like(ggain)

        def finish(rows):
            du = contract(b_g[0, 0, rows, :], local_weights(0), 1, 1)
            for l in range(2):
                part, x = du[:, columns(l)], stash[rows, columns(l)].astype(F32)
                ggain[:, columns(l)] += jnp.sum(part * x, axis=0, keepdims=True)
                value = part * gain[:, columns(l)] - x * acc[rows, :]
                grad_in[rows, columns(l)] = (ret[rows, columns(l)].astype(F32) + value).astype(BF16)

        over_rows(finish)
        yield

    def weight_grads(p, k):
        g = ret if (p == 1 and k == last) else b_g.at[p, k]
        f = p * factors + k
        for l in range(2):
            if k == 0:
                lhs = s_v[p, 0]
            else:
                lhs = jnp.concatenate([s_v[p, k, :, columns(l)], s_o[p, k - 1, :, columns(l)]], axis=1)
            both = contract(lhs, g[:, columns(l)], 0, 0).astype(BF16)
            mine, theirs = (1, 0) if (k == 0 and l == 1) else (0, 1)
            gself[f, columns(l), :] = both[columns(mine), :]
            gpart[f, columns(l), :] = both[columns(theirs), :]

    from_ahead = send(gback, ret, (behind, tp))
    from_behind = send(sent, arr, (ahead, tp))
    chains = {
        "S": forward_chain(stash, None, s_v, s_o, 0, stash_first, None, False),
        "A": forward_chain(arr, from_behind, a_v, a_o, 1, arriving_first, arriving_second, True),
        "B": backward_chain(),
    }
    for name, index in order:
        if name == "G":
            weight_grads(*index)
        else:
            next(chains[name])
    for copy in pending:
        copy.wait_send()


def make_order(bits, lag):
    steps = 2 * bits + 1
    order = []
    for t in range(steps + lag):
        if t < steps:
            order += [("S", t), ("B", t)]
        if t >= lag:
            order.append(("A", t - lag))
        if bits <= t < steps:
            order += [("G", (1, t - bits)), ("G", (0, 2 * bits - t))]
    return order


def solution(mesh):
    sections, shards = mesh.shape["section"], mesh.shape["tp"]
    bits = shards.bit_length() - 1

    def per_device(sent_act, stash, grad_back, gain, self_blocks, partner_blocks, block_mask):
        tokens, width = stash.shape[1:]
        factors = self_blocks.shape[2]
        assert width == 2 * BLOCK and factors == bits + 1
        count = 2 * factors
        mask = block_mask[0].reshape(count, 2, 1, 1).astype(BF16)
        partw = (partner_blocks[0].reshape(count, 2, BLOCK, BLOCK) * mask).reshape(count, width, BLOCK)
        copies = 2 + 6 * bits + 3 * bits
        vmem = pl.BlockSpec(memory_space=pltpu.VMEM)
        out_act, grad_in, gself, gpart, ggain = pl.pallas_call(
            functools.partial(kernel, sections, bits, make_order(bits, 2)),
            out_shape=(
                jax.ShapeDtypeStruct((tokens, width), BF16),
                jax.ShapeDtypeStruct((tokens, width), BF16),
                jax.ShapeDtypeStruct((count, width, BLOCK), BF16),
                jax.ShapeDtypeStruct((count, width, BLOCK), BF16),
                jax.ShapeDtypeStruct((1, width), F32),
            ),
            in_specs=[vmem] * 6,
            out_specs=[vmem] * 5,
            scratch_shapes=[
                pltpu.VMEM((tokens, width), BF16),
                pltpu.VMEM((tokens, width), BF16),
                pltpu.VMEM((2, factors, tokens, width), BF16),
                pltpu.VMEM((2, bits, tokens, width), BF16),
                pltpu.VMEM((2, factors, tokens, width), BF16),
                pltpu.VMEM((2, bits, tokens, width), BF16),
                pltpu.VMEM((2, factors, tokens, width), BF16),
                pltpu.VMEM((2, bits, tokens, width), BF16),
                pltpu.VMEM((2, bits, tokens, width), BF16),
                pltpu.VMEM((tokens, width), F32),
                pltpu.VMEM((tokens, width), F32),
                pltpu.VMEM((tokens, BLOCK), F32),
                pltpu.VMEM((tokens, BLOCK), F32),
                pltpu.VMEM((1, tokens), F32),
                pltpu.VMEM((3, bits + 1, 1, tokens), F32),
                pltpu.VMEM((3, bits, 1, tokens), F32),
                pltpu.SemaphoreType.DMA((copies,)),
                pltpu.SemaphoreType.DMA((copies,)),
            ],
            compiler_params=pltpu.CompilerParams(
                collective_id=0, has_side_effects=True, vmem_limit_bytes=48 * 2**20
            ),
        )(
            sent_act[0],
            stash[0],
            grad_back[0],
            gain,
            self_blocks[0].reshape(count, width, BLOCK),
            partw,
        )
        gpart = (gpart.reshape(count, 2, BLOCK, BLOCK) * mask).reshape(partner_blocks.shape)
        return out_act[None], grad_in[None], gself.reshape(self_blocks.shape), gpart, ggain

    in_specs = (
        P("section", None, "tp"),
        P("section", None, "tp"),
        P("section", None, "tp"),
        P("section", "tp"),
        P("section", None, None, "tp", None),
        P("section", None, None, "tp", None),
        P("section", None, None, "tp"),
    )
    out_specs = (
        P("section", None, "tp"),
        P("section", None, "tp"),
        P("section", None, None, "tp", None),
        P("section", None, None, "tp", None),
        P("section", "tp"),
    )
    return jax.shard_map(per_device, mesh=mesh, in_specs=in_specs, out_specs=out_specs, check_vma=False)
```

time: 560 us -> 382 us (0.68)
  the two profiles are of different devices: /device:TPU:1 before, /device:TPU:28 now
where the time goes in v2:
time: 382 us
  Pallas kernels  374 us (98%)
  local copies, waits for them, and re-layouts  3.85 us (1%)
    pallas_call x1, Pallas kernels, per_device(): pl.pallas_call(functools.partial(kernel, sections, bits, make_order(bits,...  374 us

profile of v2, /device:TPU:28, one launch (start us, length us, event | category | flops | bytes accessed | tf_op | source)
XLA Modules:
  0.0 381.7 jit_solution(18362203506799686637)
XLA Ops:
  0.6 0.0 copy-start.5
  0.6 0.7 copy-done.5
  1.3 0.1 convert_element_type.12
  1.4 0.1 copy.13
  1.5 0.1 mul.30
  1.7 0.0 copy-start
  1.7 0.0 copy-start.1
  1.7 0.0 copy-start.2
  1.7 0.0 copy-start.3
  1.7 0.0 copy-start.4
  1.7 1.7 bitcast_multiply_fusion.partw
  3.4 0.0 copy-done
  3.4 0.0 copy-done.1
  3.4 0.0 copy-done.2
  3.5 0.0 copy-done.3
  3.5 0.0 copy-done.4
  3.5 374.0 %shard_map.110 = (bf16[512,256]{1,0:T(8,128)(2,1)S(1)}, bf16[512,256]{1,0:T(8,128)(2,1)S(1)}, bf16[12,256,128]{2,1,0:T(8,128)(2,1)S(1)}, bf16[12,256,128]{2,1,0:T(8,128)(2,1)S(1)}, f32[1,256]{1,0:T(1,128)S(1)}) custom-call(bf16[512,256]{1,0:T(8,128)(2,1)S(1)} %bitcast.18, bf16[512,256]{1,0:T(8,128)(2,1)S(1)} %bitcast.19, bf16[512,256]{1,0:T(8,128)(2,1)S(1)} %bitcast.20, ...), custom_call_target="tpu_custom_call" | custom-call | tf_op jit(solution)/shard_map/pallas_call | solution.py:349
  377.5 1.4 broadcast_multiply_fusion
  378.9 0.7 copy.19
  379.6 0.7 copy.20
  380.3 0.9 copy.21
  381.1 0.6 copy.22
  (5 shorter events, 0.0 us)
Async XLA Ops:
  0.6 0.7 copy-start.5
  1.7 1.8 copy-start
  1.7 1.8 copy-start.1
  1.7 1.8 copy-start.2
  1.7 1.8 copy-start.3
  1.7 1.8 copy-start.4

commit v3 on v2

v3 whole, which is shorter than its diff:
```python
import functools

import jax
import jax.numpy as jnp
from jax import lax
from jax.experimental import pallas as pl
from jax.experimental.pallas import tpu as pltpu
from jax.sharding import PartitionSpec as P

EPSILON = 1e-05
GELU_C = 0.7978845608028654
GELU_A = 0.044715
BLOCK = 128
PARTS = 2
ORDER = ""
MESH = pl.DeviceIdType.MESH
F32 = jnp.float32
BF16 = jnp.bfloat16


def gelu_value(v):
    inner = GELU_C * (v + GELU_A * v * v * v)
    return 0.5 * v * (1.0 + jnp.tanh(inner))


def gelu_slope(v):
    inner = GELU_C * (v + GELU_A * v * v * v)
    tanh_val = jnp.tanh(inner)
    return 0.5 * (1.0 + tanh_val) + 0.5 * v * (1.0 - tanh_val * tanh_val) * GELU_C * (
        1.0 + 3.0 * GELU_A * v * v
    )


def contract(a, b, da, db):
    return lax.dot_general(a, b, (((da,), (db,)), ((), ())), preferred_element_type=F32)


def columns(l):
    return slice(l * BLOCK, (l + 1) * BLOCK)


def kernel(
    sections,
    bits,
    order,
    sent,
    stash,
    gback,
    gain,
    selfw,
    partw,
    out_act,
    grad_in,
    gself,
    gpart,
    ggain,
    arr,
    ret,
    s_v,
    s_o,
    a_v,
    a_o,
    b_g,
    b_t,
    b_o,
    own,
    pre,
    acc,
    rs_col,
    rs_row,
    st_v,
    st_o,
    far_w,
    far_out,
    far_in,
    send_sem,
    recv_sem,
):
    tokens, width = stash.shape
    part_rows = tokens // PARTS
    factors = bits + 1
    last = factors - 1
    total_width = float((2**bits) * width)
    sec = lax.axis_index("section")
    tp = lax.axis_index("tp")
    ahead = lax.rem(sec + 1, sections)
    behind = lax.rem(sec + sections - 1, sections)
    peers = []
    for j in range(bits):
        m = 2**j
        peers.append(tp + m - 2 * m * ((tp // m) % 2))

    barrier = pltpu.get_barrier_semaphore()
    for peer in peers:
        pl.semaphore_signal(barrier, inc=1, device_id=(sec, peer), device_id_type=MESH)
    for other in (ahead, behind):
        pl.semaphore_signal(barrier, inc=1, device_id=(other, tp), device_id_type=MESH)
    pl.semaphore_wait(barrier, bits + 2)

    pending = []

    def send(src, dst, where):
        n = len(pending)
        copy = pltpu.make_async_remote_copy(
            src_ref=src,
            dst_ref=dst,
            send_sem=send_sem.at[n],
            recv_sem=recv_sem.at[n],
            device_id=where,
            device_id_type=MESH,
        )
        copy.start()
        pending.append(copy)
        return copy

    def rows_of(h):
        return slice(h * part_rows, (h + 1) * part_rows)

    def local_weights(p):
        f = p * factors
        top = jnp.concatenate([selfw[f, columns(0), :], partw[f, columns(1), :]], axis=1)
        low = jnp.concatenate([partw[f, columns(0), :], selfw[f, columns(1), :]], axis=1)
        return jnp.concatenate([top, low], axis=0)

    def stacked(p, k, l):
        f = p * factors + k
        return jnp.concatenate([selfw[f, columns(l), :], partw[f, columns(l), :]], axis=0)

    def row_sums(values):
        return jnp.sum(values.T, axis=0, keepdims=True)

    def as_column(row):
        return jnp.broadcast_to(row, (BLOCK, part_rows)).T

    class Total:
        def __init__(self, slot):
            self.slot, self.at = slot, 0

        def begin(self, values):
            st_v[self.slot, 0] = row_sums(values)

        def send(self, peer):
            n = self.at
            self.copy = send(st_v.at[self.slot, n], st_o.at[self.slot, n], (sec, peer))

        def absorb(self):
            n = self.at
            self.copy.wait_recv()
            st_v[self.slot, n + 1] = st_v[self.slot, n] + st_o[self.slot, n]
            self.at = n + 1

        def value(self):
            return st_v[self.slot, self.at]

    def scale_of(total):
        return lax.rsqrt(total.value() / total_width + EPSILON)

    def forward_chain(h, x, wait_x, v, o, slot, finish_first, finish_second):
        rows = rows_of(h)

        def forward(p, k, emit):
            if k == 0:
                both = contract(v[p, 0, rows, :], local_weights(p), 1, 0)
                for l in range(2):
                    emit(l, both[:, columns(l)])
                return
            for l in range(2):
                lhs = jnp.concatenate(
                    [v[p, k, rows, columns(l)], o[p, k - 1, rows, columns(l)]], axis=1
                )
                emit(l, contract(lhs, stacked(p, k, l), 1, 0))

        def store(p, k):
            def emit(l, value):
                v[p, k, rows, columns(l)] = value.astype(BF16)

            return emit

        total = Total(slot)
        if wait_x is not None:
            wait_x.wait_recv()
        squares = None
        for l in range(2):
            part = x[rows, columns(l)].astype(F32)
            v[0, 0, rows, columns(l)] = (part * gain[:, columns(l)]).astype(BF16)
            squares = part * part if squares is None else squares + part * part
        total.begin(squares)
        for p in range(2):
            forward(p, 0, store(p, 1))
            for k in range(1, factors):
                if p == 1 and k == last and finish_second is None:
                    break
                copy = send(v.at[p, k, rows, :], o.at[p, k - 1, rows, :], (sec, peers[k - 1]))
                if p == 0:
                    total.send(peers[k - 1])
                yield
                copy.wait_recv()
                if p == 0:
                    total.absorb()
                if k < last:
                    forward(p, k, store(p, k + 1))
                elif p == 0:
                    forward(p, k, finish_first(rows, total))
                else:
                    forward(p, k, functools.partial(finish_second, rows))
        yield

    def stash_first(rows, total):
        scale = scale_of(total)
        rs_row[:, rows] = scale
        rs_col[rows, :] = as_column(scale)

        def emit(l, value):
            value = value * rs_col[rows, :]
            pre[rows, columns(l)] = value
            s_v[1, 0, rows, columns(l)] = gelu_value(value).astype(BF16)

        return emit

    def arriving_first(rows, total):
        acc[rows, :] = as_column(scale_of(total))

        def emit(l, value):
            a_v[1, 0, rows, columns(l)] = gelu_value(value * acc[rows, :]).astype(BF16)

        return emit

    def arriving_second(rows, l, value):
        out_act[rows, columns(l)] = (arr[rows, columns(l)].astype(F32) + value).astype(BF16)

    def backward_chain(h, wait_x):
        rows = rows_of(h)
        wait_x.wait_recv()
        total = Total(2 * PARTS + h)
        for p in (1, 0):
            for k in range(last, 0, -1):
                far = p == 1 and k == last
                incoming = b_o.at[p, k - 1, rows, :]
                if far:
                    copy = send(ret.at[rows, :], incoming, (sec, peers[k - 1]))
                else:
                    for l in range(2):
                        both = contract(b_g[p, k, rows, columns(l)], stacked(p, k, l), 1, 1)
                        own[rows, columns(l)] = both[:, columns(0)]
                        b_t[p, k - 1, rows, columns(l)] = both[:, columns(1)].astype(BF16)
                    copy = send(b_t.at[p, k - 1, rows, :], incoming, (sec, peers[k - 1]))
                if p == 0:
                    total.send(peers[k - 1])
                yield
                copy.wait_recv()
                if p == 0:
                    total.absorb()
                if far:
                    if h == 0:
                        far_weights.wait_recv()
                    for l in range(2):
                        lhs = jnp.concatenate(
                            [ret[rows, columns(l)], b_o[p, k - 1, rows, columns(l)]], axis=1
                        )
                        rhs = jnp.concatenate(
                            [selfw[2 * factors - 1, columns(l), :], far_w[columns(l), :]], axis=1
                        )
                        b_g[p, k - 1, rows, columns(l)] = contract(lhs, rhs, 1, 1).astype(BF16)
                else:
                    b_g[p, k - 1, rows, :] = (
                        own[rows, :] + b_o[p, k - 1, rows, :].astype(F32)
                    ).astype(BF16)
            if p == 1:
                dh = contract(b_g[1, 0, rows, :], local_weights(1), 1, 1)
                products = None
                for l in range(2):
                    a = pre[rows, columns(l)]
                    da = dh[:, columns(l)] * gelu_slope(a)
                    products = da * a if products is None else products + da * a
                    b_g[0, last, rows, columns(l)] = (da * rs_col[rows, :]).astype(BF16)
                total.begin(products)
        scale = rs_row[:, rows]
        acc[rows, :] = as_column(scale * scale * total.value() / total_width)
        du = contract(b_g[0, 0, rows, :], local_weights(0), 1, 1)
        for l in range(2):
            part, x = du[:, columns(l)], stash[rows, columns(l)].astype(F32)
            ggain[:, columns(l)] += jnp.sum(part * x, axis=0, keepdims=True)
            value = part * gain[:, columns(l)] - x * acc[rows, :]
            grad_in[rows, columns(l)] = (ret[rows, columns(l)].astype(F32) + value).astype(BF16)
        yield

    def weight_grads(p, k):
        f = p * factors + k
        for l in range(2):
            if p == 1 and k == last:
                rhs = jnp.concatenate([ret[:, columns(l)], b_o[1, last - 1, :, columns(l)]], axis=1)
                both = contract(s_v[1, last, :, columns(l)], rhs, 0, 0).astype(BF16)
                gself[f, columns(l), :] = both[:, columns(0)]
                far_out[columns(l), :] = both[:, columns(1)]
                continue
            if k == 0:
                lhs = s_v[p, 0]
            else:
                lhs = jnp.concatenate([s_v[p, k, :, columns(l)], s_o[p, k - 1, :, columns(l)]], axis=1)
            both = contract(lhs, b_g[p, k, :, columns(l)], 0, 0).astype(BF16)
            mine, theirs = (1, 0) if (k == 0 and l == 1) else (0, 1)
            gself[f, columns(l), :] = both[columns(mine), :]
            gpart[f, columns(l), :] = both[columns(theirs), :]

    far_peer = (sec, peers[last - 1])
    from_ahead, from_behind = [], []
    for h in range(PARTS):
        rows = rows_of(h)
        from_ahead.append(send(gback.at[rows, :], ret.at[rows, :], (behind, tp)))
    for h in range(PARTS):
        rows = rows_of(h)
        from_behind.append(send(sent.at[rows, :], arr.at[rows, :], (ahead, tp)))
    far_weights = send(partw.at[2 * factors - 1], far_w, far_peer)
    ggain[...] = jnp.zeros_like(ggain)
    chains = {}
    for h in range(PARTS):
        chains["S", h] = forward_chain(h, stash, None, s_v, s_o, h, stash_first, None)
        chains["A", h] = forward_chain(
            h, arr, from_behind[h], a_v, a_o, PARTS + h, arriving_first, arriving_second
        )
        chains["B", h] = backward_chain(h, from_ahead[h])
    far_grads = None
    for name, at in order:
        if name == "G":
            weight_grads(*at)
            if at == (1, last):
                far_grads = send(far_out, far_in, far_peer)
        else:
            next(chains[name, at])
    far_grads.wait_recv()
    gpart[2 * factors - 1] = far_in[...]
    for copy in pending:
        copy.wait_send()


def make_order(bits, letters):
    order = []
    done = set()
    count = {name: 0 for name in "SsAaBb"}
    grads = [(1, k) for k in range(bits + 1)] + [(0, k) for k in range(bits, -1, -1)]

    def ready(p, k):
        s, b = min(count["S"], count["s"]), min(count["B"], count["b"])
        if p == 0:
            return s > bits and b >= 2 * bits + 1 - k
        if k == bits:
            return s == 2 * bits and b >= 2
        return s >= bits + 1 + k and b >= bits + 1 - k

    for letter in letters or default_letters(bits):
        if letter == "G":
            todo = [g for g in grads if g not in done and ready(*g)]
            if todo:
                done.add(todo[0])
                order.append(("G", todo[0]))
            continue
        count[letter] += 1
        order.append((letter.upper(), int(letter.islower())))
    for g in grads:
        if g not in done:
            order.append(("G", g))
    return order


def default_letters(bits):
    letters = ""
    for t in range(2 * bits + 1):
        letters += "SBA" if t < 2 * bits else "BA"
        letters += "sba" if t < 2 * bits else "ba"
        if t >= bits:
            letters += "GG"
    return letters


def solution(mesh):
    sections, shards = mesh.shape["section"], mesh.shape["tp"]
    bits = shards.bit_length() - 1

    def per_device(sent_act, stash, grad_back, gain, self_blocks, partner_blocks, block_mask):
        tokens, width = stash.shape[1:]
        factors = self_blocks.shape[2]
        assert width == 2 * BLOCK and factors == bits + 1
        count = 2 * factors
        mask = block_mask[0].reshape(count, 2, 1, 1).astype(BF16)
        partw = (partner_blocks[0].reshape(count, 2, BLOCK, BLOCK) * mask).reshape(count, width, BLOCK)
        copies = PARTS * (2 + 9 * bits) + 2
        vmem = pl.BlockSpec(memory_space=pltpu.VMEM)
        out_act, grad_in, gself, gpart, ggain = pl.pallas_call(
            functools.partial(kernel, sections, bits, make_order(bits, ORDER)),
            out_shape=(
                jax.ShapeDtypeStruct((tokens, width), BF16),
                jax.ShapeDtypeStruct((tokens, width), BF16),
                jax.ShapeDtypeStruct((count, width, BLOCK), BF16),
                jax.ShapeDtypeStruct((count, width, BLOCK), BF16),
                jax.ShapeDtypeStruct((1, width), F32),
            ),
            in_specs=[vmem] * 6,
            out_specs=[vmem] * 5,
            scratch_shapes=[
                pltpu.VMEM((tokens, width), BF16),
                pltpu.VMEM((tokens, width), BF16),
                pltpu.VMEM((2, factors, tokens, width), BF16),
                pltpu.VMEM((2, bits, tokens, width), BF16),
                pltpu.VMEM((2, factors, tokens, width), BF16),
                pltpu.VMEM((2, bits, tokens, width), BF16),
                pltpu.VMEM((2, factors, tokens, width), BF16),
                pltpu.VMEM((2, bits, tokens, width), BF16),
                pltpu.VMEM((2, bits, tokens, width), BF16),
                pltpu.VMEM((tokens, width), F32),
                pltpu.VMEM((tokens, width), F32),
                pltpu.VMEM((tokens, BLOCK), F32),
                pltpu.VMEM((tokens, BLOCK), F32),
                pltpu.VMEM((1, tokens), F32),
                pltpu.VMEM((3 * PARTS, bits + 1, 1, tokens // PARTS), F32),
                pltpu.VMEM((3 * PARTS, bits, 1, tokens // PARTS), F32),
                pltpu.VMEM((width, BLOCK), BF16),
                pltpu.VMEM((width, BLOCK), BF16),
                pltpu.VMEM((width, BLOCK), BF16),
                pltpu.SemaphoreType.DMA((copies,)),
                pltpu.SemaphoreType.DMA((copies,)),
            ],
            compiler_params=pltpu.CompilerParams(
                collective_id=0, has_side_effects=True, vmem_limit_bytes=48 * 2**20
            ),
        )(
            sent_act[0],
            stash[0],
            grad_back[0],
            gain,
            self_blocks[0].reshape(count, width, BLOCK),
            partw,
        )
        gpart = (gpart.reshape(count, 2, BLOCK, BLOCK) * mask).reshape(partner_blocks.shape)
        return out_act[None], grad_in[None], gself.reshape(self_blocks.shape), gpart, ggain

    in_specs = (
        P("section", None, "tp"),
        P("section", None, "tp"),
        P("section", None, "tp"),
        P("section", "tp"),
        P("section", None, None, "tp", None),
        P("section", None, None, "tp", None),
        P("section", None, None, "tp"),
    )
    out_specs = (
        P("section", None, "tp"),
        P("section", None, "tp"),
        P("section", None, None, "tp", None),
        P("section", None, None, "tp", None),
        P("section", "tp"),
    )
    return jax.shard_map(per_device, mesh=mesh, in_specs=in_specs, out_specs=out_specs, check_vma=False)
```

time: 382 us -> 328 us (0.86)
  the two profiles are of different devices: /device:TPU:28 before, /device:TPU:30 now
where the time goes in v3:
time: 328 us
  Pallas kernels  320 us (98%)
  local copies, waits for them, and re-layouts  3.85 us (1%)
    pallas_call x1, Pallas kernels, per_device(): pl.pallas_call(functools.partial(kernel, sections, bits, make_order(bits,...  320 us

profile of v3, /device:TPU:30, one launch (start us, length us, event | category | flops | bytes accessed | tf_op | source)
XLA Modules:
  0.0 328.0 jit_solution(4715378879295316443)
XLA Ops:
  0.6 0.0 copy-start.5
  0.6 0.7 copy-done.5
  1.3 0.1 convert_element_type.12
  1.4 0.1 copy.13
  1.5 0.1 mul.30
  1.7 0.0 copy-start
  1.7 0.0 copy-start.1
  1.7 0.0 copy-start.2
  1.7 0.0 copy-start.3
  1.7 0.0 copy-start.4
  1.7 1.7 bitcast_multiply_fusion.partw
  3.4 0.0 copy-done
  3.4 0.0 copy-done.1
  3.4 0.0 copy-done.2
  3.5 0.0 copy-done.3
  3.5 0.0 copy-done.4
  3.5 320.3 %shard_map.110 = (bf16[512,256]{1,0:T(8,128)(2,1)S(1)}, bf16[512,256]{1,0:T(8,128)(2,1)S(1)}, bf16[12,256,128]{2,1,0:T(8,128)(2,1)S(1)}, bf16[12,256,128]{2,1,0:T(8,128)(2,1)S(1)}, f32[1,256]{1,0:T(1,128)S(1)}) custom-call(bf16[512,256]{1,0:T(8,128)(2,1)S(1)} %bitcast.18, bf16[512,256]{1,0:T(8,128)(2,1)S(1)} %bitcast.19, bf16[512,256]{1,0:T(8,128)(2,1)S(1)} %bitcast.20, ...), custom_call_target="tpu_custom_call" | custom-call | tf_op jit(solution)/shard_map/pallas_call | solution.py:388
  323.8 1.4 broadcast_multiply_fusion
  325.2 0.7 copy.19
  325.9 0.7 copy.20
  326.6 0.9 copy.21
  327.4 0.6 copy.22
  (5 shorter events, 0.0 us)
Async XLA Ops:
  0.6 0.7 copy-start.5
  1.7 1.8 copy-start
  1.7 1.8 copy-start.1
  1.7 1.8 copy-start.2
  1.7 1.8 copy-start.3
  1.7 1.8 copy-start.4

commit v4 on v3

--- a/solution.py
+++ b/solution.py
@@ -12,7 +12,14 @@
 GELU_A = 0.044715
 BLOCK = 128
 PARTS = 2
-ORDER = ""
+ORDER = "".join(
+    [
+        "SBsbSBAsbaSBAsbaSBAsbaSB",
+        "AsbaSBAsbaGGSBAsbaGGSBAs",
+        "baGGSBAsbaGGSBAsbaGGBAba",
+        "GGAaGG",
+    ]
+)
 MESH = pl.DeviceIdType.MESH
 F32 = jnp.float32
 BF16 = jnp.bfloat16
@@ -73,6 +80,9 @@
     far_w,
     far_out,
     far_in,
+    near_s,
+    near_p,
+    near_v,
     send_sem,
     recv_sem,
 ):
@@ -89,13 +99,15 @@
     for j in range(bits):
         m = 2**j
         peers.append(tp + m - 2 * m * ((tp // m) % 2))
+    m = 2 ** (bits - 2)
+    beside = peers[bits - 1] + m - 2 * m * ((tp // m) % 2)
 
     barrier = pltpu.get_barrier_semaphore()
-    for peer in peers:
+    for peer in (*peers, beside):
         pl.semaphore_signal(barrier, inc=1, device_id=(sec, peer), device_id_type=MESH)
     for other in (ahead, behind):
         pl.semaphore_signal(barrier, inc=1, device_id=(other, tp), device_id_type=MESH)
-    pl.semaphore_wait(barrier, bits + 2)
+    pl.semaphore_wait(barrier, bits + 3)
 
     pending = []
 
@@ -170,6 +182,18 @@
                 )
                 emit(l, contract(lhs, stacked(p, k, l), 1, 0))
 
+        def neighbour(p):
+            if p not in near_ready:
+                near_ready.append(p)
+                for copy in near_weights[p]:
+                    copy.wait_recv()
+            for l in range(2):
+                lhs = jnp.concatenate(
+                    [o[p, last - 2, rows, columns(l)], v[p, last - 1, rows, columns(l)]], axis=1
+                )
+                rhs = jnp.concatenate([near_s[p, columns(l), :], near_p[p, columns(l), :]], axis=0)
+                near_v[2 * slot + p, :, columns(l)] = contract(lhs, rhs, 1, 0).astype(BF16)
+
         def store(p, k):
             def emit(l, value):
                 v[p, k, rows, columns(l)] = value.astype(BF16)
@@ -186,17 +210,25 @@
             squares = part * part if squares is None else squares + part * part
         total.begin(squares)
         for p in range(2):
+            if p == 1 and p not in near_weights:
+                send_near(p)
             forward(p, 0, store(p, 1))
             for k in range(1, factors):
                 if p == 1 and k == last and finish_second is None:
                     break
-                copy = send(v.at[p, k, rows, :], o.at[p, k - 1, rows, :], (sec, peers[k - 1]))
+                if k == last:
+                    src, where = near_v.at[2 * slot + p], beside
+                else:
+                    src, where = v.at[p, k, rows, :], peers[k - 1]
+                copy = send(src, o.at[p, k - 1, rows, :], (sec, where))
                 if p == 0:
-                    total.send(peers[k - 1])
+                    total.send(where)
                 yield
                 copy.wait_recv()
                 if p == 0:
                     total.absorb()
+                if k == last - 1 and not (p == 1 and finish_second is None):
+                    neighbour(p)
                 if k < last:
                     forward(p, k, store(p, k + 1))
                 elif p == 0:
@@ -311,6 +343,16 @@
         rows = rows_of(h)
         from_behind.append(send(sent.at[rows, :], arr.at[rows, :], (ahead, tp)))
     far_weights = send(partw.at[2 * factors - 1], far_w, far_peer)
+    near_weights, near_ready = {}, []
+
+    def send_near(p):
+        f, where = p * factors + last - 1, (sec, peers[last - 2])
+        near_weights[p] = (
+            send(selfw.at[f], near_s.at[p], where),
+            send(partw.at[f], near_p.at[p], where),
+        )
+
+    send_near(0)
     ggain[...] = jnp.zeros_like(ggain)
     chains = {}
     for h in range(PARTS):
@@ -383,7 +425,7 @@
         count = 2 * factors
         mask = block_mask[0].reshape(count, 2, 1, 1).astype(BF16)
         partw = (partner_blocks[0].reshape(count, 2, BLOCK, BLOCK) * mask).reshape(count, width, BLOCK)
-        copies = PARTS * (2 + 9 * bits) + 2
+        copies = PARTS * (2 + 9 * bits) + 6
         vmem = pl.BlockSpec(memory_space=pltpu.VMEM)
         out_act, grad_in, gself, gpart, ggain = pl.pallas_call(
             functools.partial(kernel, sections, bits, make_order(bits, ORDER)),
@@ -416,6 +458,9 @@
                 pltpu.VMEM((width, BLOCK), BF16),
                 pltpu.VMEM((width, BLOCK), BF16),
                 pltpu.VMEM((width, BLOCK), BF16),
+                pltpu.VMEM((2, width, BLOCK), BF16),
+                pltpu.VMEM((2, width, BLOCK), BF16),
+                pltpu.VMEM((4 * PARTS, tokens // PARTS, width), BF16),
                 pltpu.SemaphoreType.DMA((copies,)),
                 pltpu.SemaphoreType.DMA((copies,)),
             ],

time: 328 us -> 306 us (0.933)
  the two profiles are of different devices: /device:TPU:30 before, /device:TPU:139 now
where the time goes in v4:
time: 306 us
  Pallas kernels  298 us (97%)
  local copies, waits for them, and re-layouts  3.85 us (1%)
  other arithmetic  3.07 us (1%)
    pallas_call x1, Pallas kernels, per_device(): pl.pallas_call(functools.partial(kernel, sections, bits, make_order(bits,...  298 us

profile of v4, /device:TPU:139, one launch (start us, length us, event | category | flops | bytes accessed | tf_op | source)
XLA Modules:
  0.0 305.9 jit_solution(2605003148484230918)
XLA Ops:
  0.6 0.0 copy-start.5
  0.6 0.7 copy-done.5
  1.3 0.1 convert_element_type.12
  1.4 0.1 copy.13
  1.5 0.1 mul.30
  1.7 0.0 copy-start
  1.7 0.0 copy-start.1
  1.7 0.0 copy-start.2
  1.7 0.0 copy-start.3
  1.7 0.0 copy-start.4
  1.7 1.7 bitcast_multiply_fusion.partw
  3.4 0.0 copy-done
  3.4 0.0 copy-done.1
  3.4 0.0 copy-done.2
  3.5 0.0 copy-done.3
  3.5 0.0 copy-done.4
  3.5 298.2 %shard_map.110 = (bf16[512,256]{1,0:T(8,128)(2,1)S(1)}, bf16[512,256]{1,0:T(8,128)(2,1)S(1)}, bf16[12,256,128]{2,1,0:T(8,128)(2,1)S(1)}, bf16[12,256,128]{2,1,0:T(8,128)(2,1)S(1)}, f32[1,256]{1,0:T(1,128)S(1)}) custom-call(bf16[512,256]{1,0:T(8,128)(2,1)S(1)} %bitcast.18, bf16[512,256]{1,0:T(8,128)(2,1)S(1)} %bitcast.19, bf16[512,256]{1,0:T(8,128)(2,1)S(1)} %bitcast.20, ...), custom_call_target="tpu_custom_call" | custom-call | tf_op jit(solution)/shard_map/pallas_call | solution.py:430
  301.7 1.4 broadcast_multiply_fusion
  303.1 0.7 copy.19
  303.8 0.7 copy.20
  304.5 0.9 copy.21
  305.3 0.6 copy.22
  (5 shorter events, 0.0 us)
Async XLA Ops:
  0.6 0.7 copy-start.5
  1.7 1.8 copy-start
  1.7 1.8 copy-start.1
  1.7 1.8 copy-start.2
  1.7 1.8 copy-start.3
  1.7 1.8 copy-start.4

commit v5 on v4

--- a/solution.py
+++ b/solution.py
@@ -55,7 +55,8 @@
     gback,
     gain,
     selfw,
-    partw,
+    raw_partw,
+    present,
     out_act,
     grad_in,
     gself,
@@ -83,6 +84,7 @@
     near_s,
     near_p,
     near_v,
+    partw,
     send_sem,
     recv_sem,
 ):
@@ -342,6 +344,10 @@
     for h in range(PARTS):
         rows = rows_of(h)
         from_behind.append(send(sent.at[rows, :], arr.at[rows, :], (ahead, tp)))
+    for f in range(2 * factors):
+        for l in range(2):
+            blocks = raw_partw[f, columns(l), :].astype(F32)
+            partw[f, columns(l), :] = (blocks * present[f, l].astype(F32)).astype(BF16)
     far_weights = send(partw.at[2 * factors - 1], far_w, far_peer)
     near_weights, near_ready = {}, []
 
@@ -424,7 +430,6 @@
         assert width == 2 * BLOCK and factors == bits + 1
         count = 2 * factors
         mask = block_mask[0].reshape(count, 2, 1, 1).astype(BF16)
-        partw = (partner_blocks[0].reshape(count, 2, BLOCK, BLOCK) * mask).reshape(count, width, BLOCK)
         copies = PARTS * (2 + 9 * bits) + 6
         vmem = pl.BlockSpec(memory_space=pltpu.VMEM)
         out_act, grad_in, gself, gpart, ggain = pl.pallas_call(
@@ -436,7 +441,7 @@
                 jax.ShapeDtypeStruct((count, width, BLOCK), BF16),
                 jax.ShapeDtypeStruct((1, width), F32),
             ),
-            in_specs=[vmem] * 6,
+            in_specs=[vmem] * 6 + [pl.BlockSpec(memory_space=pltpu.SMEM)],
             out_specs=[vmem] * 5,
             scratch_shapes=[
                 pltpu.VMEM((tokens, width), BF16),
@@ -461,6 +466,7 @@
                 pltpu.VMEM((2, width, BLOCK), BF16),
                 pltpu.VMEM((2, width, BLOCK), BF16),
                 pltpu.VMEM((4 * PARTS, tokens // PARTS, width), BF16),
+                pltpu.VMEM((count, width, BLOCK), BF16),
                 pltpu.SemaphoreType.DMA((copies,)),
                 pltpu.SemaphoreType.DMA((copies,)),
             ],
@@ -473,7 +479,8 @@
             grad_back[0],
             gain,
             self_blocks[0].reshape(count, width, BLOCK),
-            partw,
+            partner_blocks[0].reshape(count, width, BLOCK),
+            block_mask[0].reshape(count, 2),
         )
         gpart = (gpart.reshape(count, 2, BLOCK, BLOCK) * mask).reshape(partner_blocks.shape)
         return out_act[None], grad_in[None], gself.reshape(self_blocks.shape), gpart, ggain

time: 306 us -> 310 us (1.013)
  the two profiles are of different devices: /device:TPU:139 before, /device:TPU:136 now
where the time goes in v5:
time: 310 us; the launch traced here: 309 us
  Pallas kernels  298 us (96%)
  local copies, waits for them, and re-layouts  9.58 us (3%)
    pallas_call x1, Pallas kernels, per_device(): pl.pallas_call(functools.partial(kernel, sections, bits, make_order(bits,...  298 us
    unnamed x19, local copies, waits for them, and re-layouts  9.22 us

profile of v5, /device:TPU:136, one launch (start us, length us, event | category | flops | bytes accessed | tf_op | source)
XLA Modules:
  0.0 309.3 jit_solution(11902208924917256214)
XLA Ops:
  0.6 0.0 copy-start.6
  0.6 0.7 copy-done.6
  1.3 0.1 reshape_squeeze.12
  1.4 0.1 copy.14
  1.5 0.1 mul.19
  1.6 0.0 copy-start.5
  1.6 0.1 copy.13.present
  1.7 0.6 copy-done.5
  2.3 0.0 copy-start
  2.3 1.1 copy-done
  3.4 0.0 copy-start.1
  3.4 1.1 copy-done.1
  4.6 0.0 copy-start.2
  4.6 0.9 copy-done.2
  5.5 0.0 copy-start.3
  5.5 0.9 copy-done.3
  6.5 0.0 copy-start.4
  6.5 0.9 copy-done.4
  7.4 297.6 %shard_map.110 = (bf16[512,256]{1,0:T(8,128)(2,1)S(1)}, bf16[512,256]{1,0:T(8,128)(2,1)S(1)}, bf16[12,256,128]{2,1,0:T(8,128)(2,1)S(1)}, bf16[12,256,128]{2,1,0:T(8,128)(2,1)S(1)}, f32[1,256]{1,0:T(1,128)S(1)}) custom-call(bf16[512,256]{1,0:T(8,128)(2,1)S(1)} %bitcast.15, bf16[512,256]{1,0:T(8,128)(2,1)S(1)} %bitcast.16, bf16[512,256]{1,0:T(8,128)(2,1)S(1)} %bitcast.17, ...), custom_call_target="tpu_custom_call" | custom-call | tf_op jit(solution)/shard_map/pallas_call | solution.py:435
  305.1 1.4 broadcast_multiply_fusion
  306.4 0.7 copy.19
  307.1 0.7 copy.20
  307.8 0.9 copy.21
  308.7 0.6 copy.22
  (3 shorter events, 0.0 us)
Async XLA Ops:
  0.6 0.7 copy-start.6
  1.6 0.7 copy-start.5
  2.3 1.1 copy-start
  3.4 1.1 copy-start.1
  4.6 0.9 copy-start.2
  5.5 0.9 copy-start.3
  6.5 0.9 copy-start.4
